TPU v7x, 128 devices: a whole 4x4x4 slice. The times are simulated.
128 devices in a mesh: section: 4 (over x), expert: 32 (over z, y, core).
Axes of the slice: x: 4, y: 4, z: 4, core: 2. Of those that a mesh axis runs over, the one named last changes fastest.
Arguments:
- upstream: bfloat16 [4, 4096, 3584], P('section', 'expert'), may hold values from -0.59765625 to 0.59765625
- routes: int32 [4, 4096, 2], P('section', 'expert'), may hold values from 0 to 7, all different within a row; in each aligned block of 128 rows (0 to 127, 128 to 255, ..., all dimensions but the last counted through in order) at most 48 rows name the same one
- gates: float32 [4, 4096, 2], P('section', 'expert'), may hold values from 0.1 to 1
- w_gate: bfloat16 [4, 3584, 8192], P('section', None, 'expert'), may hold values from -0.09375 to 0.09375
- w_up: bfloat16 [4, 3584, 8192], P('section', None, 'expert'), may hold values from -0.09375 to 0.09375
- w_down: bfloat16 [4, 8192, 3584], P('section', 'expert'), may hold values from -0.1875 to 0.1875
- stash_q: bfloat16 [4, 49152, 3584], P('section', 'expert'), may hold values from -448 to 448
- stash_scale: float32 [4, 49152, 28], P('section', 'expert'), may hold values from 0.004 to 0.04
Outputs:
- grad_input: bfloat16 [4, 4096, 3584], P('section', 'expert')
- grad_gates: float32 [4, 4096, 2], P('section', 'expert')
- grad_w_gate: bfloat16 [4, 3584, 8192], P('section', None, 'expert')
- grad_w_up: bfloat16 [4, 3584, 8192], P('section', None, 'expert')
- grad_w_down: bfloat16 [4, 8192, 3584], P('section', 'expert')
Inputs may be any that keep to these rules, and one draw needn't show every extreme that they name: `routes`: in each section, each token names 2 different experts, and within the 128 tokens of one device no expert is named more than 48 times; some expert is named exactly 48 times.
All inputs are finite; a program needn't handle non-finite values.
Results may differ from a plain program's by a relative error of at most 0.014.
Values may be sent and summed in bfloat16 or wider, within the bound.
A program may use at most 256 MiB of HBM per device.

v0:
```python
import functools

import jax
import jax.numpy as jnp
from jax import lax
from jax.experimental import pallas as pl
from jax.experimental.pallas import tpu as pltpu
from jax.sharding import PartitionSpec as P

EXPERTS = 8
CAP = 48
NCHIP = 16
NDEV = 32
CH = 256
D = 3584
HALF = D // 2
NK = HALF // CH
SLOTS = NDEV * CAP
FD = 256
TOK = 128
FR = 256
NFR = SLOTS // FR
QR = 64
MESH = pl.DeviceIdType.MESH
BF = jnp.bfloat16
F32 = jnp.float32


def dot(a, b, ca, cb):
    return lax.dot_general(a, b, (((ca,), (cb,)), ((), ())), preferred_element_type=F32)


def wait_bytes(ref, sem):
    pltpu.make_async_copy(ref, ref, sem).wait()


def kernel(
    nsec,
    routes, gates, up, wg_h, wu_h, wd_h, sq_h, ss_h,
    gi_h, gg_o, gwg_h, gwu_h, gwd_h,
    rows, inputs, wg, wu, wd, ga, gb, hid, raw, sh, dg, du,
    send, xbuf, comb, psend, back, gout, gsib, scale, gmat, tgt,
    gsend, grecv, gpsend, gprecv, st_d, st_g, st_u,
    x_send, x_recv, d_send, d_recv, s_send, s_recv, p_send, p_recv,
    c_send, c_recv, gm_send, gm_recv, g_send, g_recv, gp_send, gp_recv,
    gi_send, gi_recv, w_sem, sq_sem, ss_sem, o_sem, go_sem,
):
    sec = lax.axis_index("section")
    me = lax.axis_index("expert")
    chip = me // 2
    core = me % 2
    sib = me + 1 - 2 * core
    other = 1 - core
    down = (sec + nsec - 1) % nsec
    upper = (sec + 1) % nsec

    pltpu.make_async_copy(ss_h, scale, ss_sem).start()
    for r in range(NFR):
        pltpu.make_async_copy(
            sq_h.at[pl.ds(r * FR, FR)], inputs.at[pl.ds(r * FR, FR)], sq_sem.at[r]
        ).start()
    pltpu.make_async_copy(wg_h, wg, w_sem.at[0]).start()
    pltpu.make_async_copy(wu_h, wu, w_sem.at[1]).start()
    for j in range(2 * NK):
        pltpu.make_async_copy(wd_h.at[:, pl.ds(j * CH, CH)], wd.at[j], w_sem.at[2 + j]).start()

    bar = pltpu.get_barrier_semaphore()

    def greet(o, _):
        pl.semaphore_signal(
            bar, inc=1, device_id=(sec, (me + o) % NDEV), device_id_type=MESH
        )
        return 0

    lax.fori_loop(1, NDEV, greet, 0)
    for sx in (down, upper):
        for cc in range(2):
            pl.semaphore_signal(
                bar, inc=1, device_id=(sx, chip * 2 + cc), device_id_type=MESH
            )
    pl.semaphore_wait(bar, NDEV - 1 + 4)

    def xs(k, _):
        for cc in range(2):
            pltpu.make_async_remote_copy(
                src_ref=up.at[:, pl.ds(pl.multiple_of(cc * HALF + k * CH, CH), CH)],
                dst_ref=xbuf.at[k, core],
                send_sem=x_send,
                recv_sem=x_recv.at[k],
                device_id=(down, chip * 2 + cc),
                device_id_type=MESH,
            ).start()
        return 0

    lax.fori_loop(0, NK, xs, 0)

    lane = lax.broadcasted_iota(jnp.int32, (TOK, TOK), 1)
    sub = lax.broadcasted_iota(jnp.int32, (TOK, TOK), 0)
    r0 = routes[:, 0:1]
    r1 = routes[:, 1:2]
    o0 = (lane == r0).astype(F32)
    o1 = (lane == r1).astype(F32)
    lower = (lane < sub).astype(BF)
    before = dot(lower, (o0 + o1).astype(BF), 1, 0)
    t0 = r0 * CAP + jnp.sum(before * o0, axis=1, keepdims=True).astype(jnp.int32)
    t1 = r1 * CAP + jnp.sum(before * o1, axis=1, keepdims=True).astype(jnp.int32)
    tgt[0] = jnp.broadcast_to(t0, (TOK, TOK))
    tgt[1] = jnp.broadcast_to(t1, (TOK, TOK))
    wide = lax.broadcasted_iota(jnp.int32, (TOK, EXPERTS * CAP), 1)
    gmat[core] = ((wide == t0) | (wide == t1)).astype(F32).astype(BF)
    for e in range(EXPERTS):
        at = lane + e * CAP
        inside = lane < CAP
        hit = jnp.where((at == t0) & inside, gates[:, 0:1], 0.0) + jnp.where(
            (at == t1) & inside, gates[:, 1:2], 0.0
        )
        gsend[e] = jnp.broadcast_to(jnp.sum(hit, axis=0, keepdims=True), (8, TOK))
    pltpu.make_async_remote_copy(
        src_ref=gmat.at[core], dst_ref=gmat.at[core], send_sem=gm_send, recv_sem=gm_recv,
        device_id=(sec, sib), device_id_type=MESH,
    ).start()

    def sendg(o, _):
        to = (me + o) % NDEV
        pltpu.make_async_remote_copy(
            src_ref=gsend.at[to // 4], dst_ref=grecv.at[me], send_sem=g_send,
            recv_sem=g_recv, device_id=(sec, to), device_id_type=MESH,
        ).start()
        return 0

    lax.fori_loop(1, NDEV, sendg, 0)
    pltpu.make_async_copy(gsend.at[me // 4], grecv.at[me], g_recv).start()
    wait_bytes(gmat.at[0], gm_recv)

    pltpu.make_async_copy(ss_h, scale, ss_sem).wait()
    pltpu.make_async_copy(wg_h, wg, w_sem.at[0]).wait()
    pltpu.make_async_copy(wu_h, wu, w_sem.at[1]).wait()

    def dispatch(k, _):
        wait_bytes(xbuf.at[k], x_recv.at[k])
        for b in range(2):
            packed = dot(gmat[b], xbuf[k, b], 0, 0).astype(BF)
            send[k, :, b] = packed.reshape(EXPERTS, CAP, CH)

        def out(o, _):
            to = (chip + o) % NCHIP
            pltpu.make_async_remote_copy(
                src_ref=send.at[k, to // 2],
                dst_ref=rows.at[core * NK + k, pl.ds(chip * 2, 2)],
                send_sem=d_send.at[k], recv_sem=d_recv.at[k],
                device_id=(sec, to * 2 + core), device_id_type=MESH,
            ).start()
            return 0

        lax.fori_loop(1, NCHIP, out, 0)
        pltpu.make_async_copy(
            send.at[k, chip // 2], rows.at[core * NK + k, pl.ds(chip * 2, 2)], d_recv.at[k]
        ).start()

        @pl.when(k < NFR)
        def _():
            base = pl.multiple_of(k * FR, FR)
            wait_bytes(inputs.at[pl.ds(base, FR)], sq_sem.at[k])

            def dequant(q, _):
                at = pl.multiple_of(base + q * QR, QR)
                sc = scale[pl.ds(at, QR), :]
                for n in range(D // 128):
                    cols = slice(n * 128, (n + 1) * 128)
                    v = inputs[pl.ds(at, QR), cols].astype(F32) * sc[:, n : n + 1]
                    inputs[pl.ds(at, QR), cols] = v.astype(BF)
                return 0

            lax.fori_loop(0, FR // QR, dequant, 0)
            ga[pl.ds(base, FR)] = dot(inputs[pl.ds(base, FR)], wg[...], 1, 0)
            gb[pl.ds(base, FR)] = dot(inputs[pl.ds(base, FR)], wu[...], 1, 0)

        return 0

    lax.fori_loop(0, NK, dispatch, 0)

    wait_bytes(grecv, g_recv)
    diag = lax.broadcasted_iota(jnp.int32, (CAP, TOK), 0) == lax.broadcasted_iota(
        jnp.int32, (CAP, TOK), 1
    )

    def factors(b, _):
        at = pl.ds(pl.multiple_of(b * CAP, CAP), CAP)
        w = jnp.sum(jnp.where(diag, grecv[b][0:1], 0.0), axis=1, keepdims=True)
        g = ga[at]
        u = gb[at]
        sigma = jax.nn.sigmoid(g)
        swish = g * sigma
        h = swish * u
        hid[at] = h
        sh[at] = (w * h).astype(BF)
        ga[at] = w * u * sigma * (1.0 + g * (1.0 - sigma))
        gb[at] = w * swish
        return 0

    lax.fori_loop(0, NDEV, factors, 0)
    for j in range(2 * NK):
        pltpu.make_async_copy(
            wd_h.at[:, pl.ds(j * CH, CH)], wd.at[j], w_sem.at[2 + j]
        ).wait()
    raw[...] = jnp.zeros_like(raw)

    def add_raw(j):
        def part(r, _):
            at = pl.ds(pl.multiple_of(r * 384, 384), 384)
            blk = rows[j, pl.ds(r * 8, 8)].reshape(384, CH)
            raw[at] += dot(blk, wd[j], 1, 1)
            return 0

        lax.fori_loop(0, 4, part, 0)

    def arrive(k, _):
        mine = core * NK + k
        theirs = other * NK + k
        wait_bytes(rows.at[mine], d_recv.at[k])
        pltpu.make_async_remote_copy(
            src_ref=rows.at[mine], dst_ref=rows.at[mine], send_sem=s_send.at[k],
            recv_sem=s_recv.at[k], device_id=(sec, sib), device_id_type=MESH,
        ).start()
        add_raw(mine)
        wait_bytes(rows.at[theirs], s_recv.at[k])
        add_raw(theirs)
        return 0

    lax.fori_loop(0, NK, arrive, 0)

    def pre(b, _):
        at = pl.ds(pl.multiple_of(b * CAP, CAP), CAP)
        r = raw[at]
        dg[at] = (r * ga[at]).astype(BF)
        du[at] = (r * gb[at]).astype(BF)
        part = jnp.sum(r * hid[at], axis=1, keepdims=True)
        line = jnp.sum(jnp.where(diag, part, 0.0), axis=0, keepdims=True)
        gpsend[b] = jnp.broadcast_to(line, (8, TOK))
        return 0

    lax.fori_loop(0, NDEV, pre, 0)

    def partial_of(j, r):
        at = pl.ds(pl.multiple_of(r * 384, 384), 384)
        feat = pl.ds(pl.multiple_of(j * CH, CH), CH)
        return dot(dg[at], wg[feat], 1, 1) + dot(du[at], wu[feat], 1, 1)

    def to_sibling(k):
        slot = k % 2

        @pl.when(k >= 2)
        def _():
            wait_bytes(psend.at[slot], p_send.at[slot])

        def part(r, _):
            psend[slot, pl.ds(r * 8, 8)] = (
                partial_of(other * NK + k, r).astype(BF).reshape(8, CAP, CH)
            )
            return 0

        lax.fori_loop(0, 4, part, 0)
        pltpu.make_async_remote_copy(
            src_ref=psend.at[slot], dst_ref=comb.at[k], send_sem=p_send.at[slot],
            recv_sem=p_recv.at[k], device_id=(sec, sib), device_id_type=MESH,
        ).start()

    to_sibling(0)
    self_at = (chip % 2) * 8 + chip // 2

    def combine(k, _):
        @pl.when(k + 1 < NK)
        def _():
            to_sibling(k + 1)

        wait_bytes(comb.at[k], p_recv.at[k])

        def part(r, _):
            got = comb[k, pl.ds(r * 8, 8)].reshape(384, CH).astype(F32)
            comb[k, pl.ds(r * 8, 8)] = (
                (partial_of(core * NK + k, r) + got).astype(BF).reshape(8, CAP, CH)
            )
            return 0

        lax.fori_loop(0, 4, part, 0)

        def out(o, _):
            to = (chip + o) % NCHIP
            pltpu.make_async_remote_copy(
                src_ref=comb.at[k, pl.ds(to * 2, 2)],
                dst_ref=back.at[k, self_at],
                send_sem=c_send.at[k], recv_sem=c_recv.at[k],
                device_id=(sec, to * 2 + core), device_id_type=MESH,
            ).start()
            return 0

        lax.fori_loop(1, NCHIP, out, 0)
        pltpu.make_async_copy(
            comb.at[k, pl.ds(chip * 2, 2)], back.at[k, self_at], c_recv.at[k]
        ).start()
        return 0

    lax.fori_loop(0, NK, combine, 0)

    def sendgp(o, _):
        to = (me + o) % NDEV
        pltpu.make_async_remote_copy(
            src_ref=gpsend.at[to], dst_ref=gprecv.at[me], send_sem=gp_send,
            recv_sem=gp_recv, device_id=(sec, to), device_id_type=MESH,
        ).start()
        return 0

    lax.fori_loop(1, NDEV, sendgp, 0)
    pltpu.make_async_copy(gpsend.at[me], gprecv.at[me], gp_recv).start()

    def outs(slot, j):
        feat = pl.ds(pl.multiple_of(j * CH, CH), CH)
        return (
            pltpu.make_async_copy(st_d.at[slot], gwd_h.at[:, feat], o_sem.at[0, slot]),
            pltpu.make_async_copy(st_g.at[slot], gwg_h.at[feat], o_sem.at[1, slot]),
            pltpu.make_async_copy(st_u.at[slot], gwu_h.at[feat], o_sem.at[2, slot]),
        )

    def wgrad(j, _):
        slot = j % 2

        @pl.when(j >= 2)
        def _():
            for copy in outs(slot, j - 2):
                copy.wait()

        feat = pl.ds(pl.multiple_of(j * CH, CH), CH)
        st_d[slot] = dot(sh[...], rows[j].reshape(SLOTS, CH), 0, 0).astype(BF)
        st_g[slot] = dot(inputs[:, feat], dg[...], 0, 0).astype(BF)
        st_u[slot] = dot(inputs[:, feat], du[...], 0, 0).astype(BF)
        for copy in outs(slot, j):
            copy.start()
        return 0

    lax.fori_loop(0, 2 * NK, wgrad, 0)
    for j in (2 * NK - 2, 2 * NK - 1):
        for copy in outs(j % 2, j):
            copy.wait()

    def unpack(b, k):
        even = back[k, 0:8, b].reshape(EXPERTS * CAP, CH)
        odd = back[k, 8:16, b].reshape(EXPERTS * CAP, CH)
        return (dot(gmat[b], even, 1, 0) + dot(gmat[b], odd, 1, 0)).astype(BF)

    def final(k, _):
        wait_bytes(back.at[k], c_recv.at[k])
        gsib[k] = unpack(other, k)
        pltpu.make_async_remote_copy(
            src_ref=gsib.at[k], dst_ref=gout.at[core * NK + k], send_sem=gi_send,
            recv_sem=gi_recv.at[k], device_id=(sec, sib), device_id_type=MESH,
        ).start()
        gout[core * NK + k] = unpack(core, k)
        return 0

    lax.fori_loop(0, NK, final, 0)

    wait_bytes(gprecv, gp_recv)
    acc0 = jnp.zeros((TOK, TOK), F32)
    acc1 = jnp.zeros((TOK, TOK), F32)
    for e in range(EXPERTS):
        total = (
            gprecv[4 * e][0:1] + gprecv[4 * e + 1][0:1]
            + gprecv[4 * e + 2][0:1] + gprecv[4 * e + 3][0:1]
        )
        at = lane + e * CAP
        inside = lane < CAP
        acc0 = acc0 + jnp.where((at == tgt[0]) & inside, total, 0.0)
        acc1 = acc1 + jnp.where((at == tgt[1]) & inside, total, 0.0)
    gg_o[:, 0:1] = jnp.sum(acc0, axis=1, keepdims=True)
    gg_o[:, 1:2] = jnp.sum(acc1, axis=1, keepdims=True)

    def write(k, _):
        wait_bytes(gout.at[other * NK + k], gi_recv.at[k])
        return 0

    lax.fori_loop(0, NK, write, 0)
    for j in range(2 * NK):
        pltpu.make_async_copy(
            gout.at[j], gi_h.at[:, pl.ds(j * CH, CH)], go_sem.at[j]
        ).start()

    wait_bytes(xbuf, x_send)
    wait_bytes(gmat.at[0], gm_send)
    wait_bytes(grecv.at[pl.ds(0, NDEV - 1)], g_send)
    wait_bytes(gprecv.at[pl.ds(0, NDEV - 1)], gp_send)
    wait_bytes(gsib, gi_send)

    def drain(k, _):
        wait_bytes(rows.at[k, pl.ds(0, 30)], d_send.at[k])
        wait_bytes(comb.at[k, pl.ds(0, 30)], c_send.at[k])
        wait_bytes(rows.at[k], s_send.at[k])
        return 0

    lax.fori_loop(0, NK, drain, 0)
    for slot in range(2):
        wait_bytes(psend.at[slot], p_send.at[slot])
    for j in range(2 * NK):
        pltpu.make_async_copy(
            gout.at[j], gi_h.at[:, pl.ds(j * CH, CH)], go_sem.at[j]
        ).wait()


def local(nsec, upstream, routes, gates, w_gate, w_up, w_down, stash_q, stash_scale):
    hbm = pl.BlockSpec(memory_space=pl.ANY)
    vmem = pl.BlockSpec(memory_space=pltpu.VMEM)
    dma = pltpu.SemaphoreType.DMA
    v = pltpu.VMEM
    scratch = [
        v((2 * NK, NDEV, CAP, CH), BF),
        v((SLOTS, D), BF),
        v((D, FD), BF), v((D, FD), BF), v((2 * NK, FD, CH), BF),
        v((SLOTS, FD), F32), v((SLOTS, FD), F32), v((SLOTS, FD), F32), v((SLOTS, FD), F32),
        v((SLOTS, FD), BF), v((SLOTS, FD), BF), v((SLOTS, FD), BF),
        v((NK, EXPERTS, 2, CAP, CH), BF),
        v((NK, 2, TOK, CH), BF),
        v((NK, NDEV, CAP, CH), BF),
        v((2, NDEV, CAP, CH), BF),
        v((NK, NCHIP, 2, CAP, CH), BF),
        v((2 * NK, TOK, CH), BF), v((NK, TOK, CH), BF),
        v((SLOTS, D // 128), F32),
        v((2, TOK, EXPERTS * CAP), BF),
        v((2, TOK, TOK), jnp.int32),
        v((EXPERTS, 8, TOK), F32), v((NDEV, 8, TOK), F32),
        v((NDEV, 8, TOK), F32), v((NDEV, 8, TOK), F32),
        v((2, FD, CH), BF), v((2, CH, FD), BF), v((2, CH, FD), BF),
        dma, dma((NK,)), dma((NK,)), dma((NK,)), dma((NK,)), dma((NK,)),
        dma((2,)), dma((NK,)), dma((NK,)), dma((NK,)), dma, dma, dma, dma, dma, dma,
        dma, dma((NK,)), dma((2 + 2 * NK,)), dma((NFR,)), dma, dma((3, 2)), dma((2 * NK,)),
    ]
    out = pl.pallas_call(
        functools.partial(kernel, nsec),
        out_shape=(
            jax.ShapeDtypeStruct((TOK, D), BF),
            jax.ShapeDtypeStruct((TOK, 2), F32),
            jax.ShapeDtypeStruct((D, FD), BF),
            jax.ShapeDtypeStruct((D, FD), BF),
            jax.ShapeDtypeStruct((FD, D), BF),
        ),
        in_specs=[vmem, vmem] + [hbm] * 6,
        out_specs=(hbm, vmem, hbm, hbm, hbm),
        scratch_shapes=scratch,
        compiler_params=pltpu.CompilerParams(
            collective_id=0, has_side_effects=True, vmem_limit_bytes=66_000_000
        ),
    )(
        routes[0], gates[0], upstream[0], w_gate[0], w_up[0], w_down[0],
        stash_q[0], stash_scale[0],
    )
    return tuple(o[None] for o in out)


def solution(mesh):
    three = P("section", "expert", None)
    cols = P("section", None, "expert")
    return jax.shard_map(
        functools.partial(local, mesh.shape["section"]),
        mesh=mesh,
        in_specs=(three, three, three, cols, cols, three, three, three),
        out_specs=(three, three, cols, cols, three),
        check_vma=False,
    )
```

profile of v0, /device:TPU:1, one launch (start us, length us, event | category | flops | bytes accessed | tf_op | source)
XLA Modules:
  0.0 173.0 jit_solution(16603934157073453812)
XLA Ops:
  0.6 1.4 copy.13
  2.0 1.4 copy.14
  3.5 2.1 %copy.15 = f32[1,1536,28]{2,1,0:T(8,128)} copy(f32[1,1536,28]{1,0,2:T(1,128)} %param.15) | data formatting | bytes 344064 | tf_op args[7]
  5.5 158.1 %shard_map.119 = (bf16[128,3584]{1,0:T(8,128)(2,1)}, f32[128,2]{1,0:T(8,128)}, bf16[3584,256]{1,0:T(8,128)(2,1)}, bf16[3584,256]{1,0:T(8,128)(2,1)}, bf16[256,3584]{1,0:T(8,128)(2,1)}) custom-call(s32[128,2]{1,0:T(8,128)} %bitcast.23, f32[128,2]{1,0:T(8,128)} %bitcast.24, bf16[128,3584]{1,0:T(8,128)(2,1)} %bitcast.22, bf16[3584,256]{1,0:T(8,128)(2,1)} %bitcast.15, ...), custom_call_target="tpu_custom_call" | custom-call | tf_op jit(solution)/shard_map/pallas_call | solution.py:435
  163.7 0.0 copy-start.2
  163.7 1.6 copy.16
  165.3 2.2 %copy.21 = bf16[1,128,3584]{2,1,0:T(8,128)(2,1)} copy(bf16[1,128,3584]{2,1,0:T(8,128)(2,1)} %bitcast.21) | data formatting | bytes 1835008
  167.5 0.0 copy-done.2
  167.5 0.0 copy-start.1
  167.5 1.2 copy.22
  168.7 0.9 copy-done.1
  169.6 0.0 copy-start
  169.6 1.2 copy.23
  170.9 0.9 copy-done
  171.8 1.2 copy.24
Async XLA Ops:
  163.7 3.8 %copy-start.2 = (bf16[3584,256]{1,0:T(8,128)(2,1)S(1)}, bf16[3584,256]{1,0:T(8,128)(2,1)}, u32[]{:S(2)}) copy-start(bf16[3584,256]{1,0:T(8,128)(2,1)} %get-tuple-element.12) | copy-start | bytes 5505028
  167.5 2.2 %copy-start.1 = (bf16[3584,256]{1,0:T(8,128)(2,1)S(1)}, bf16[3584,256]{1,0:T(8,128)(2,1)}, u32[]{:S(2)}) copy-start(bf16[3584,256]{1,0:T(8,128)(2,1)} %get-tuple-element.13) | copy-start | bytes 5505028
  169.6 2.2 %copy-start = (bf16[256,3584]{1,0:T(8,128)(2,1)S(1)}, bf16[256,3584]{1,0:T(8,128)(2,1)}, u32[]{:S(2)}) copy-start(bf16[256,3584]{1,0:T(8,128)(2,1)} %get-tuple-element.14) | copy-start | bytes 5505028
where the time goes:
time: 174 us; the launch traced here: 173 us
  Pallas kernels  158 us (91%)
  local copies, waits for them, and re-layouts  14.2 us (8%)
    pallas_call x1, Pallas kernels, local(): pl.pallas_call(functools.partial(kernel, nsec), out_shape=(jax.ShapeDtype...  158 us
    unnamed x14, local copies, waits for them, and re-layouts  14.2 us

commit v1 on v0

v1 whole, which is shorter than its diff:
```python
import functools

import jax
import jax.numpy as jnp
from jax import lax
from jax.experimental import pallas as pl
from jax.experimental.pallas import tpu as pltpu
from jax.sharding import PartitionSpec as P

EXPERTS = 8
CAP = 48
NCHIP = 16
NDEV = 32
CH = 256
D = 3584
HALF = D // 2
NK = HALF // CH
SLOTS = NDEV * CAP
FD = 256
TOK = 128
NFR = 8
HSLOTS = SLOTS // 2
PART = HSLOTS // 2
MESH = pl.DeviceIdType.MESH
BF = jnp.bfloat16
F32 = jnp.float32


def dot(a, b, ca, cb):
    return lax.dot_general(a, b, (((ca,), (cb,)), ((), ())), preferred_element_type=F32)


def wait_bytes(ref, sem):
    pltpu.make_async_copy(ref, ref, sem).wait()


def kernel(
    nsec,
    routes, gates, up, wg_h, wu_h, wd_h, sq_h, ss_h,
    gi_h, gg_o, gwg_h, gwu_h, gwd_h,
    rows, inputs, wg, wu, wd, ga, gb, hid, raw, sh, dg, du,
    send, xbuf, comb, psend, back, gout, gsib, scale, scale_t, gmat, tgt,
    gsend, grecv, gpsend, gprecv, st_d, st_g, st_u,
    x_send, x_recv, d_send, d_recv, s_send, s_recv, p_send, p_recv,
    c_send, c_recv, gm_send, gm_recv, g_send, g_recv, gp_send, gp_recv,
    gi_send, gi_recv, w_sem, sq_sem, ss_sem, o_sem, go_sem,
):
    sec = lax.axis_index("section")
    me = lax.axis_index("expert")
    chip = me // 2
    core = me % 2
    sib = me + 1 - 2 * core
    other = 1 - core
    down = (sec + nsec - 1) % nsec
    upper = (sec + 1) % nsec

    pltpu.make_async_copy(ss_h, scale, ss_sem).start()

    def stash(f):
        return pltpu.make_async_copy(
            sq_h.at[pl.ds((f % 4) * 4, 4), f // 4],
            inputs.at[f // 4, pl.ds((f % 4) * 4, 4)],
            sq_sem.at[f],
        )

    for f in range(NFR):
        stash(f).start()
    pltpu.make_async_copy(wg_h, wg, w_sem.at[0]).start()
    pltpu.make_async_copy(wu_h, wu, w_sem.at[1]).start()
    for j in range(2 * NK):
        pltpu.make_async_copy(wd_h.at[:, pl.ds(j * CH, CH)], wd.at[j], w_sem.at[2 + j]).start()

    bar = pltpu.get_barrier_semaphore()

    def greet(o, _):
        pl.semaphore_signal(
            bar, inc=1, device_id=(sec, (me + o) % NDEV), device_id_type=MESH
        )
        return 0

    lax.fori_loop(1, NDEV, greet, 0)
    for sx in (down, upper):
        for cc in range(2):
            pl.semaphore_signal(
                bar, inc=1, device_id=(sx, chip * 2 + cc), device_id_type=MESH
            )

    lane = lax.broadcasted_iota(jnp.int32, (TOK, TOK), 1)
    sub = lax.broadcasted_iota(jnp.int32, (TOK, TOK), 0)
    same = lane == sub

    def column(row):
        return jnp.sum(jnp.where(same, row, 0), axis=1, keepdims=True)

    r0 = column(routes[0:1, :])
    r1 = column(routes[1:2, :])
    w0 = column(gates[0:1, :])
    w1 = column(gates[1:2, :])
    o0 = (lane == r0).astype(F32)
    o1 = (lane == r1).astype(F32)
    lower = (lane < sub).astype(BF)
    before = dot(lower, (o0 + o1).astype(BF), 1, 0)
    t0 = r0 * CAP + jnp.sum(before * o0, axis=1, keepdims=True).astype(jnp.int32)
    t1 = r1 * CAP + jnp.sum(before * o1, axis=1, keepdims=True).astype(jnp.int32)
    tgt[0] = jnp.broadcast_to(t0, (TOK, TOK))
    tgt[1] = jnp.broadcast_to(t1, (TOK, TOK))
    wide = lax.broadcasted_iota(jnp.int32, (TOK, EXPERTS * CAP), 1)
    gmat[core] = ((wide == t0) | (wide == t1)).astype(F32).astype(BF)
    for e in range(EXPERTS):
        at = lane + e * CAP
        inside = lane < CAP
        hit = jnp.where((at == t0) & inside, w0, 0.0) + jnp.where((at == t1) & inside, w1, 0.0)
        gsend[e] = jnp.broadcast_to(jnp.sum(hit, axis=0, keepdims=True), (8, TOK))

    pl.semaphore_wait(bar, NDEV - 1 + 4)

    def xs(k, _):
        for cc in range(2):
            pltpu.make_async_remote_copy(
                src_ref=up.at[:, pl.ds(pl.multiple_of(cc * HALF + k * CH, CH), CH)],
                dst_ref=xbuf.at[k, core],
                send_sem=x_send,
                recv_sem=x_recv.at[k],
                device_id=(down, chip * 2 + cc),
                device_id_type=MESH,
            ).start()
        return 0

    pltpu.make_async_remote_copy(
        src_ref=gmat.at[core], dst_ref=gmat.at[core], send_sem=gm_send, recv_sem=gm_recv,
        device_id=(sec, sib), device_id_type=MESH,
    ).start()
    lax.fori_loop(0, NK, xs, 0)

    def sendg(o, _):
        to = (me + o) % NDEV
        pltpu.make_async_remote_copy(
            src_ref=gsend.at[to // 4], dst_ref=grecv.at[me], send_sem=g_send,
            recv_sem=g_recv, device_id=(sec, to), device_id_type=MESH,
        ).start()
        return 0

    lax.fori_loop(1, NDEV, sendg, 0)
    pltpu.make_async_copy(gsend.at[me // 4], grecv.at[me], g_recv).start()

    pltpu.make_async_copy(ss_h, scale, ss_sem).wait()
    for q in range(4):
        for m in range(3):
            at = slice(q * 384 + m * 128, q * 384 + (m + 1) * 128)
            lines = [scale[n, :, at] for n in range(D // 128)]
            lines.append(jnp.zeros((4, 128), F32))
            scale_t[at, :] = jnp.concatenate(lines, axis=0).T
    wait_bytes(gmat.at[0], gm_recv)

    pltpu.make_async_copy(wg_h, wg, w_sem.at[0]).wait()
    pltpu.make_async_copy(wu_h, wu, w_sem.at[1]).wait()

    def spread(h, k):
        def out(o, _):
            to = (chip + o) % NCHIP
            pltpu.make_async_remote_copy(
                src_ref=send.at[k, h, to // 2],
                dst_ref=rows.at[core * NK + k, h, chip],
                send_sem=d_send.at[h * NK + k], recv_sem=d_recv.at[h * NK + k],
                device_id=(sec, to * 2 + core), device_id_type=MESH,
            ).start()
            return 0

        lax.fori_loop(1, NCHIP, out, 0)
        pltpu.make_async_copy(
            send.at[k, h, chip // 2], rows.at[core * NK + k, h, chip], d_recv.at[h * NK + k]
        ).start()

    def forward(f):
        h = f // 4
        c4 = (f % 4) * 4
        stash(f).wait()

        def dequant(q, _):
            chp = c4 + q
            sc = scale_t[pl.ds(pl.multiple_of((chp * 2 + h) * CAP, CAP), CAP), :]
            for n in range(D // 128):
                cols = slice(n * 128, (n + 1) * 128)
                v = inputs[h, chp, :, cols].astype(F32) * sc[:, n : n + 1]
                inputs[h, chp, :, cols] = v.astype(BF)
            return 0

        lax.fori_loop(0, 4, dequant, 0)
        at = pl.ds(pl.multiple_of(f * 4 * CAP, 4 * CAP), 4 * CAP)
        block = inputs[h, pl.ds(c4, 4)].reshape(4 * CAP, D)
        ga[at] = dot(block, wg[...], 1, 0)
        gb[at] = dot(block, wu[...], 1, 0)

    def dispatch(k, _):
        wait_bytes(xbuf.at[k], x_recv.at[k])
        for b in range(2):
            packed = dot(gmat[b], xbuf[k, b], 0, 0).astype(BF)
            send[k, b] = packed.reshape(EXPERTS, CAP, CH)
        spread(0, k)
        forward(k)
        return 0

    lax.fori_loop(0, NK, dispatch, 0)

    def dispatch1(k, _):
        spread(1, k)
        return 0

    lax.fori_loop(0, NK, dispatch1, 0)
    forward(NK)

    wait_bytes(grecv, g_recv)
    diag = lax.broadcasted_iota(jnp.int32, (CAP, TOK), 0) == lax.broadcasted_iota(
        jnp.int32, (CAP, TOK), 1
    )

    def factors(b, _):
        at = pl.ds(pl.multiple_of(b * CAP, CAP), CAP)
        source = (b % NCHIP) * 2 + b // NCHIP
        w = jnp.sum(jnp.where(diag, grecv[source][0:1], 0.0), axis=1, keepdims=True)
        g = ga[at]
        u = gb[at]
        sigma = jax.nn.sigmoid(g)
        swish = g * sigma
        h = swish * u
        hid[at] = h
        sh[at] = (w * h).astype(BF)
        ga[at] = w * u * sigma * (1.0 + g * (1.0 - sigma))
        gb[at] = w * swish
        return 0

    lax.fori_loop(0, NDEV, factors, 0)
    for j in range(2 * NK):
        pltpu.make_async_copy(
            wd_h.at[:, pl.ds(j * CH, CH)], wd.at[j], w_sem.at[2 + j]
        ).wait()
    raw[...] = jnp.zeros_like(raw)

    def add_raw(h, j):
        def part(r, _):
            at = pl.ds(pl.multiple_of(h * HSLOTS + r * PART, PART), PART)
            blk = rows[j, h, pl.ds(r * 8, 8)].reshape(PART, CH)
            raw[at] += dot(blk, wd[j], 1, 1)
            return 0

        lax.fori_loop(0, 2, part, 0)

    def arrive(h, k):
        mine = core * NK + k
        theirs = other * NK + k
        t = h * NK + k
        wait_bytes(rows.at[mine, h], d_recv.at[t])
        pltpu.make_async_remote_copy(
            src_ref=rows.at[mine, h], dst_ref=rows.at[mine, h], send_sem=s_send.at[t],
            recv_sem=s_recv.at[t], device_id=(sec, sib), device_id_type=MESH,
        ).start()
        add_raw(h, mine)
        wait_bytes(rows.at[theirs, h], s_recv.at[t])
        add_raw(h, theirs)

    def pre(b, _):
        at = pl.ds(pl.multiple_of(b * CAP, CAP), CAP)
        r = raw[at]
        dg[at] = (r * ga[at]).astype(BF)
        du[at] = (r * gb[at]).astype(BF)
        part = jnp.sum(r * hid[at], axis=1, keepdims=True)
        line = jnp.sum(jnp.where(diag, part, 0.0), axis=0, keepdims=True)
        gpsend[(b % NCHIP) * 2 + b // NCHIP] = jnp.broadcast_to(line, (8, TOK))
        return 0

    def partial_of(h, j, r):
        at = pl.ds(pl.multiple_of(h * HSLOTS + r * PART, PART), PART)
        feat = pl.ds(pl.multiple_of(j * CH, CH), CH)
        return dot(dg[at], wg[feat], 1, 1) + dot(du[at], wu[feat], 1, 1)

    def to_sibling(h, k):
        t = h * NK + k
        slot = t % 2

        @pl.when(t >= 2)
        def _():
            wait_bytes(psend.at[slot], p_send.at[slot])

        def part(r, _):
            psend[slot, pl.ds(r * 8, 8)] = (
                partial_of(h, other * NK + k, r).astype(BF).reshape(8, CAP, CH)
            )
            return 0

        lax.fori_loop(0, 2, part, 0)
        pltpu.make_async_remote_copy(
            src_ref=psend.at[slot], dst_ref=comb.at[h, k], send_sem=p_send.at[slot],
            recv_sem=p_recv.at[t], device_id=(sec, sib), device_id_type=MESH,
        ).start()

    self_at = (chip % 2) * 8 + chip // 2

    def combine(h, k):
        t = h * NK + k

        @pl.when(k + 1 < NK)
        def _():
            to_sibling(h, k + 1)

        wait_bytes(comb.at[h, k], p_recv.at[t])

        def part(r, _):
            got = comb[h, k, pl.ds(r * 8, 8)].reshape(PART, CH).astype(F32)
            comb[h, k, pl.ds(r * 8, 8)] = (
                (partial_of(h, core * NK + k, r) + got).astype(BF).reshape(8, CAP, CH)
            )
            return 0

        lax.fori_loop(0, 2, part, 0)

        def out(o, _):
            to = (chip + o) % NCHIP
            pltpu.make_async_remote_copy(
                src_ref=comb.at[h, k, to],
                dst_ref=back.at[h, k, self_at],
                send_sem=c_send.at[t], recv_sem=c_recv.at[t],
                device_id=(sec, to * 2 + core), device_id_type=MESH,
            ).start()
            return 0

        lax.fori_loop(1, NCHIP, out, 0)
        pltpu.make_async_copy(
            comb.at[h, k, chip], back.at[h, k, self_at], c_recv.at[t]
        ).start()

    def half(h, _):
        def arrivals(k, _):
            arrive(h, k)
            return 0

        lax.fori_loop(0, NK, arrivals, 0)
        lax.fori_loop(h * NCHIP, h * NCHIP + NCHIP, pre, 0)
        to_sibling(h, 0)

        def combines(k, _):
            combine(h, k)
            return 0

        lax.fori_loop(0, NK, combines, 0)
        return 0

    lax.fori_loop(0, 2, half, 0)

    def sendgp(o, _):
        to = (me + o) % NDEV
        pltpu.make_async_remote_copy(
            src_ref=gpsend.at[to], dst_ref=gprecv.at[me], send_sem=gp_send,
            recv_sem=gp_recv, device_id=(sec, to), device_id_type=MESH,
        ).start()
        return 0

    lax.fori_loop(1, NDEV, sendgp, 0)
    pltpu.make_async_copy(gpsend.at[me], gprecv.at[me], gp_recv).start()

    def outs(slot, j):
        feat = pl.ds(pl.multiple_of(j * CH, CH), CH)
        return (
            pltpu.make_async_copy(st_d.at[slot], gwd_h.at[:, feat], o_sem.at[0, slot]),
            pltpu.make_async_copy(st_g.at[slot], gwg_h.at[feat], o_sem.at[1, slot]),
            pltpu.make_async_copy(st_u.at[slot], gwu_h.at[feat], o_sem.at[2, slot]),
        )

    def wgrad(j, _):
        slot = j % 2

        @pl.when(j >= 2)
        def _():
            for copy in outs(slot, j - 2):
                copy.wait()

        feat = pl.ds(pl.multiple_of(j * CH, CH), CH)
        st_d[slot] = dot(sh[...], rows[j].reshape(SLOTS, CH), 0, 0).astype(BF)
        xin = inputs[:, :, :, feat].reshape(SLOTS, CH)
        st_g[slot] = dot(xin, dg[...], 0, 0).astype(BF)
        st_u[slot] = dot(xin, du[...], 0, 0).astype(BF)
        for copy in outs(slot, j):
            copy.start()
        return 0

    lax.fori_loop(0, 2 * NK, wgrad, 0)
    for j in (2 * NK - 2, 2 * NK - 1):
        for copy in outs(j % 2, j):
            copy.wait()

    def final(h, k):
        wait_bytes(back.at[h, k], c_recv.at[h * NK + k])
        even = back[h, k, 0:8].reshape(EXPERTS * CAP, CH)
        odd = back[h, k, 8:16].reshape(EXPERTS * CAP, CH)
        got = (dot(gmat[h], even, 1, 0) + dot(gmat[h], odd, 1, 0)).astype(BF)

        @pl.when(core == h)
        def _():
            gout[core * NK + k] = got

        @pl.when(core != h)
        def _():
            gsib[k] = got
            pltpu.make_async_remote_copy(
                src_ref=gsib.at[k], dst_ref=gout.at[core * NK + k], send_sem=gi_send,
                recv_sem=gi_recv.at[k], device_id=(sec, sib), device_id_type=MESH,
            ).start()

    for h in range(2):

        def finals(k, _):
            final(h, k)
            return 0

        lax.fori_loop(0, NK, finals, 0)

    def put(j):
        return pltpu.make_async_copy(
            gout.at[j], gi_h.at[:, pl.ds(pl.multiple_of(j * CH, CH), CH)], go_sem.at[j]
        )

    def write(k, _):
        put(core * NK + k).start()
        return 0

    lax.fori_loop(0, NK, write, 0)

    wait_bytes(gprecv, gp_recv)
    acc0 = jnp.zeros((TOK, TOK), F32)
    acc1 = jnp.zeros((TOK, TOK), F32)
    for e in range(EXPERTS):
        total = (
            gprecv[4 * e][0:1] + gprecv[4 * e + 1][0:1]
            + gprecv[4 * e + 2][0:1] + gprecv[4 * e + 3][0:1]
        )
        at = lane + e * CAP
        inside = lane < CAP
        acc0 = acc0 + jnp.where((at == tgt[0]) & inside, total, 0.0)
        acc1 = acc1 + jnp.where((at == tgt[1]) & inside, total, 0.0)
    for n, acc in enumerate((acc0, acc1)):
        part = jnp.sum(acc, axis=1, keepdims=True)
        gg_o[n : n + 1, :] = jnp.sum(jnp.where(same, part, 0.0), axis=0, keepdims=True)

    def write_sib(k, _):
        wait_bytes(gout.at[other * NK + k], gi_recv.at[k])
        put(other * NK + k).start()
        return 0

    lax.fori_loop(0, NK, write_sib, 0)

    wait_bytes(xbuf, x_send)
    wait_bytes(gmat.at[0], gm_send)
    wait_bytes(grecv.at[pl.ds(0, NDEV - 1)], g_send)
    wait_bytes(gprecv.at[pl.ds(0, NDEV - 1)], gp_send)
    wait_bytes(gsib, gi_send)

    def drain(t, _):
        wait_bytes(rows.at[0, 0, pl.ds(0, NCHIP - 1)], d_send.at[t])
        wait_bytes(comb.at[0, 0, pl.ds(0, NCHIP - 1)], c_send.at[t])
        wait_bytes(rows.at[0, 0], s_send.at[t])
        put(t).wait()
        return 0

    lax.fori_loop(0, 2 * NK, drain, 0)
    for slot in range(2):
        wait_bytes(psend.at[slot], p_send.at[slot])


def emit(*refs):
    count = (len(refs) - 1) // 3
    srcs, dsts, bufs, sem = refs[:count], refs[count : 2 * count], refs[2 * count : -1], refs[-1]
    loads, stores = [], []
    n = 0
    for src, dst, buf in zip(srcs, dsts, bufs):
        size = src.shape[0]
        pieces = 4 if size >= 64 else 1
        for p in range(pieces):
            at = pl.ds(p * (size // pieces), size // pieces)
            loads.append(pltpu.make_async_copy(src.at[at], buf.at[at], sem.at[0, n]))
            stores.append(pltpu.make_async_copy(buf.at[at], dst.at[at], sem.at[1, n]))
            n += 1
    for load in loads:
        load.start()
    for load, store in zip(loads, stores):
        load.wait()
        store.start()
    for store in stores:
        store.wait()


def local(nsec, upstream, routes, gates, w_gate, w_up, w_down, stash_q, stash_scale):
    hbm = pl.BlockSpec(memory_space=pl.ANY)
    vmem = pl.BlockSpec(memory_space=pltpu.VMEM)
    dma = pltpu.SemaphoreType.DMA
    v = pltpu.VMEM
    both = 2 * NK
    scratch = [
        v((both, 2, NCHIP, CAP, CH), BF),
        v((2, NCHIP, CAP, D), BF),
        v((D, FD), BF), v((D, FD), BF), v((both, FD, CH), BF),
        v((SLOTS, FD), F32), v((SLOTS, FD), F32), v((SLOTS, FD), F32), v((SLOTS, FD), F32),
        v((SLOTS, FD), BF), v((SLOTS, FD), BF), v((SLOTS, FD), BF),
        v((NK, 2, EXPERTS, CAP, CH), BF),
        v((NK, 2, TOK, CH), BF),
        v((2, NK, NCHIP, CAP, CH), BF),
        v((2, NCHIP, CAP, CH), BF),
        v((2, NK, NCHIP, CAP, CH), BF),
        v((both, TOK, CH), BF), v((NK, TOK, CH), BF),
        v((D // 128, 1, SLOTS), F32), v((SLOTS, 32), F32),
        v((2, TOK, EXPERTS * CAP), BF),
        v((2, TOK, TOK), jnp.int32),
        v((EXPERTS, 8, TOK), F32), v((NDEV, 8, TOK), F32),
        v((NDEV, 8, TOK), F32), v((NDEV, 8, TOK), F32),
        v((2, FD, CH), BF), v((2, CH, FD), BF), v((2, CH, FD), BF),
        dma, dma((NK,)), dma((both,)), dma((both,)), dma((both,)), dma((both,)),
        dma((2,)), dma((both,)), dma((both,)), dma((both,)), dma, dma, dma, dma, dma, dma,
        dma, dma((NK,)), dma((2 + both,)), dma((NFR,)), dma, dma((3, 2)), dma((both,)),
    ]
    shapes = (
        jax.ShapeDtypeStruct((TOK, D), BF),
        jax.ShapeDtypeStruct((2, TOK), F32),
        jax.ShapeDtypeStruct((D, FD), BF),
        jax.ShapeDtypeStruct((D, FD), BF),
        jax.ShapeDtypeStruct((FD, D), BF),
    )
    out = pl.pallas_call(
        functools.partial(kernel, nsec),
        out_shape=shapes,
        in_specs=[vmem, vmem] + [hbm] * 6,
        out_specs=(hbm, vmem, hbm, hbm, hbm),
        scratch_shapes=scratch,
        compiler_params=pltpu.CompilerParams(
            collective_id=0, has_side_effects=True, vmem_limit_bytes=66_000_000
        ),
    )(
        routes[0].T, gates[0].T, upstream[0], w_gate[0], w_up[0], w_down[0],
        stash_q.reshape(NCHIP, 2, CAP, D), jnp.transpose(stash_scale, (2, 0, 1)),
    )
    out = pl.pallas_call(
        emit,
        out_shape=shapes,
        in_specs=[hbm] * 5,
        out_specs=(hbm,) * 5,
        scratch_shapes=[v(o.shape, o.dtype) for o in shapes] + [dma((2, 20))],
        compiler_params=pltpu.CompilerParams(vmem_limit_bytes=64_000_000),
    )(*out)
    gi, gg, gwg, gwu, gwd = out
    return gi[None], gg.T[None], gwg[None], gwu[None], gwd[None]


def solution(mesh):
    three = P("section", "expert", None)
    cols = P("section", None, "expert")
    return jax.shard_map(
        functools.partial(local, mesh.shape["section"]),
        mesh=mesh,
        in_specs=(three, three, three, cols, cols, three, three, three),
        out_specs=(three, three, cols, cols, three),
        check_vma=False,
    )
```

time: 174 us -> 146 us (0.84)
  local copies, waits for them, and re-layouts: 14.2 us -> 0 us
  Pallas kernels: 158 us -> 145 us
    unnamed x14 -> x0, local copies, waits for them, and re-layouts: 14.2 us -> none
    pallas_call x1 -> x2, Pallas kernels: 158 us -> 145 us  [the longest x1 140 us: local(): pl.pallas_call(functools.partial(kernel, nsec), out_shape=shapes, in_spec...]
where the time goes in v1:
time: 146 us
  Pallas kernels  145 us (99%)
    pallas_call x1, Pallas kernels, local(): pl.pallas_call(functools.partial(kernel, nsec), out_shape=shapes, in_spec...  140 us
    pallas_call x1, Pallas kernels, local(): pl.pallas_call(emit, out_shape=shapes, in_specs=[hbm] * 5, out_specs=(hbm...  5.56 us

profile of v1, /device:TPU:1, one launch (start us, length us, event | category | flops | bytes accessed | tf_op | source)
XLA Modules:
  0.0 145.9 jit_solution(2409720027631741550)
XLA Ops:
  0.6 139.7 %shard_map.119 = (bf16[128,3584]{1,0:T(8,128)(2,1)}, f32[2,128]{1,0:T(2,128)}, bf16[3584,256]{1,0:T(8,128)(2,1)}, bf16[3584,256]{1,0:T(8,128)(2,1)}, bf16[256,3584]{1,0:T(8,128)(2,1)}) custom-call(s32[2,128]{1,0:T(2,128)} %bitcast.25, f32[2,128]{1,0:T(2,128)} %bitcast.26, bf16[128,3584]{1,0:T(8,128)(2,1)} %bitcast.23, bf16[3584,256]{1,0:T(8,128)(2,1)} %bitcast.20, ...), custom_call_target="tpu_custom_call" | custom-call | tf_op jit(solution)/shard_map/pallas_call | solution.py:525
  140.3 5.6 %shard_map.120 = (bf16[128,3584]{1,0:T(8,128)(2,1)}, f32[2,128]{1,0:T(2,128)}, bf16[3584,256]{1,0:T(8,128)(2,1)}, bf16[3584,256]{1,0:T(8,128)(2,1)}, bf16[256,3584]{1,0:T(8,128)(2,1)}) custom-call(bf16[128,3584]{1,0:T(8,128)(2,1)} %get-tuple-element.15.refs_0_, f32[2,128]{1,0:T(2,128)} %get-tuple-element.16.refs_1_, ...), custom_call_target="tpu_custom_call" | custom-call | tf_op jit(solution)/shard_map/pallas_call | solution.py:538

commit v2 on v1

v2 whole, which is shorter than its diff:
```python
import functools

import jax
import jax.numpy as jnp
from jax import lax
from jax.experimental import pallas as pl
from jax.experimental.pallas import tpu as pltpu
from jax.sharding import PartitionSpec as P

EXPERTS = 8
CAP = 48
NCHIP = 16
NDEV = 32
CH = 256
D = 3584
HALF = D // 2
NK = HALF // CH
NZ = 3
NY = NK - NZ
SIDE = 4
SLOTS = NDEV * CAP
FD = 256
TOK = 128
NFR = 8
HSLOTS = SLOTS // 2
PART = HSLOTS // 2
MESH = pl.DeviceIdType.MESH
BF = jnp.bfloat16
F32 = jnp.float32


def dot(a, b, ca, cb):
    return lax.dot_general(a, b, (((ca,), (cb,)), ((), ())), preferred_element_type=F32)


def wait_bytes(ref, sem):
    pltpu.make_async_copy(ref, ref, sem).wait()


def kernel(
    nsec,
    routes, gates, up, wg_h, wu_h, wd_h, sq_h, ss_h,
    gi_h, gg_o, gwg_h, gwu_h, gwd_h,
    rows, inputs, wgu, wd, ga, gb, hid, sh, dgu,
    zsend, zbuf, ybuf, ysend, xbuf, comb, psend, cbuf, backz, ybk, ytok, gout, gsib,
    scale, scale_t, gmat, gmat_t, gy, gy_t, tgt, trow, trows,
    gsend, grecv, gpsend, gprecv, st_d, st_g, st_u,
    x_send, x_recv, f_send, f_recv, d_send, d_recv, s_send, s_recv, p_send, p_recv,
    q_send, q_recv, c_send, c_recv, t_send, t_recv, g_send, g_recv, gp_send, gp_recv,
    gi_send, gi_recv, w_sem, sq_sem, ss_sem, o_sem, go_sem,
):
    sec = lax.axis_index("section")
    me = lax.axis_index("expert")
    chip = me // 2
    core = me % 2
    sib = me + 1 - 2 * core
    other = 1 - core
    down = (sec + nsec - 1) % nsec
    upper = (sec + 1) % nsec
    z = chip // SIDE
    y = chip % SIDE
    pair = y // 2

    def chunk(i):
        return i // 2 + NZ * (1 - i % 2)

    def send_to(src, dst, ssem, rsem, dev):
        pltpu.make_async_remote_copy(
            src_ref=src, dst_ref=dst, send_sem=ssem, recv_sem=rsem,
            device_id=(sec, dev), device_id_type=MESH,
        ).start()

    def at_z(zz):
        return (zz * SIDE + y) * 2 + core

    def at_y(yy):
        return (z * SIDE + yy) * 2 + core

    def others(body):
        def step(o, _):
            body(o)
            return 0

        lax.fori_loop(1, SIDE, step, 0)

    def feat(j):
        return pl.ds(pl.multiple_of(j * CH, CH), CH)

    def block(h, j):
        return rows.at[h, :, :, :, feat(j)]

    def loop(lo, hi, *steps):
        def body(i, _):
            for step in steps:
                step(i)
            return 0

        lax.fori_loop(lo, hi, body, 0)

    def by_type(i, do_y, do_z):
        if isinstance(i, int):
            (do_z if i % 2 else do_y)(i // 2)
            return

        @pl.when(i % 2 == 0)
        def _():
            do_y(i // 2)

        @pl.when(i % 2 == 1)
        def _():
            do_z(i // 2)

    pltpu.make_async_copy(ss_h, scale, ss_sem).start()

    def stash(f):
        return pltpu.make_async_copy(
            sq_h.at[pl.ds((f % 4) * 4, 4), f // 4],
            inputs.at[f // 4, pl.ds((f % 4) * 4, 4)],
            sq_sem.at[f],
        )

    for f in range(NFR):
        stash(f).start()
    weights = (
        pltpu.make_async_copy(wg_h, wgu.at[:, pl.ds(0, FD)], w_sem.at[0]),
        pltpu.make_async_copy(wu_h, wgu.at[:, pl.ds(FD, FD)], w_sem.at[1]),
        pltpu.make_async_copy(wd_h, wd, w_sem.at[2]),
    )
    for copy in weights:
        copy.start()

    bar = pltpu.get_barrier_semaphore()

    def greet(o, _):
        pl.semaphore_signal(
            bar, inc=1, device_id=(sec, (me + o) % NDEV), device_id_type=MESH
        )
        return 0

    lax.fori_loop(1, NDEV, greet, 0)
    for sx in (down, upper):
        for cc in range(2):
            pl.semaphore_signal(
                bar, inc=1, device_id=(sx, chip * 2 + cc), device_id_type=MESH
            )

    lane = lax.broadcasted_iota(jnp.int32, (TOK, TOK), 1)
    sub = lax.broadcasted_iota(jnp.int32, (TOK, TOK), 0)
    same = lane == sub

    def column(row):
        return jnp.sum(jnp.where(same, row, 0), axis=1, keepdims=True)

    r0 = column(routes[0:1, :])
    r1 = column(routes[1:2, :])
    w0 = column(gates[0:1, :])
    w1 = column(gates[1:2, :])
    o0 = (lane == r0).astype(F32)
    o1 = (lane == r1).astype(F32)
    lower = (lane < sub).astype(BF)
    before = dot(lower, (o0 + o1).astype(BF), 1, 0)
    t0 = r0 * CAP + jnp.sum(before * o0, axis=1, keepdims=True).astype(jnp.int32)
    t1 = r1 * CAP + jnp.sum(before * o1, axis=1, keepdims=True).astype(jnp.int32)
    tgt[0] = jnp.broadcast_to(t0, (TOK, TOK))
    tgt[1] = jnp.broadcast_to(t1, (TOK, TOK))
    trow[...] = jnp.zeros_like(trow)
    for n, t in enumerate((t0, t1)):
        line = jnp.sum(jnp.where(same, t, 0), axis=0, keepdims=True)
        trow[n : n + 1, :] = line.astype(F32)
    for e in range(EXPERTS):
        at = lane + e * CAP
        inside = lane < CAP
        hit = jnp.where((at == t0) & inside, w0, 0.0) + jnp.where((at == t1) & inside, w1, 0.0)
        gsend[e] = jnp.broadcast_to(jnp.sum(hit, axis=0, keepdims=True), (8, TOK))

    pl.semaphore_wait(bar, NDEV - 1 + 4)

    def xs(i):
        k = chunk(i)
        for cc in range(2):
            pltpu.make_async_remote_copy(
                src_ref=up.at[:, pl.ds(pl.multiple_of(cc * HALF + k * CH, CH), CH)],
                dst_ref=xbuf.at[k, core],
                send_sem=x_send,
                recv_sem=x_recv.at[core * NK + k],
                device_id=(down, chip * 2 + cc),
                device_id_type=MESH,
            ).start()

    @pl.when(core == 0)
    def _():
        loop(0, NK, xs)

    spot = me % 8

    def send_rows(o, _):
        to = z * 8 + (spot + o) % 8
        send_to(trow, trows.at[spot], t_send, t_recv, to)
        return 0

    lax.fori_loop(1, 8, send_rows, 0)
    pltpu.make_async_copy(trow, trows.at[spot], t_recv).start()
    def sendg(o, _):
        to = (me + o) % NDEV
        pltpu.make_async_remote_copy(
            src_ref=gsend.at[to // 4], dst_ref=grecv.at[me], send_sem=g_send,
            recv_sem=g_recv, device_id=(sec, to), device_id_type=MESH,
        ).start()
        return 0

    lax.fori_loop(1, NDEV, sendg, 0)
    pltpu.make_async_copy(gsend.at[me // 4], grecv.at[me], g_recv).start()

    def arrived(h, i):
        k = chunk(i)
        wait_bytes(xbuf.at[k, h], x_recv.at[h * NK + k])

    def first_y(h, ky):
        src = xbuf.at[NZ + ky, h]
        dst = ybuf.at[ky, h, y]
        t = h * NK + NZ + ky
        others(lambda o: send_to(src, dst, f_send.at[t], f_recv.at[t], at_y((y + o) % SIDE)))
        pltpu.make_async_copy(src, dst, f_recv.at[t]).start()

    def first_z(h, kz):
        packed = dot(gmat_t[h], xbuf[kz, h], 1, 0).astype(BF)
        zsend[kz, h] = packed.reshape(SIDE, 2, CAP, CH)
        dst = zbuf.at[kz, h, z]
        t = h * NK + kz

        def out(o):
            to = (z + o) % SIDE
            send_to(zsend.at[kz, h, to], dst, f_send.at[t], f_recv.at[t], at_z(to))

        others(out)
        pltpu.make_async_copy(zsend.at[kz, h, z], dst, f_recv.at[t]).start()

    def first(h, i):
        arrived(h, i)
        by_type(i, functools.partial(first_y, h), functools.partial(first_z, h))

    first(0, 0)

    pltpu.make_async_copy(ss_h, scale, ss_sem).wait()
    for q in range(4):
        for m in range(3):
            at = slice(q * 384 + m * 128, q * 384 + (m + 1) * 128)
            lines = [scale[n, :, at] for n in range(D // 128)]
            lines.append(jnp.zeros((4, 128), F32))
            scale_t[at, :] = jnp.concatenate(lines, axis=0).T

    wait_bytes(trows, t_recv)

    def hits(t, axis, size, positions):
        shape = (size, TOK) if axis == 0 else (TOK, size)
        at = positions(lax.broadcasted_iota(jnp.int32, shape, axis))
        lines = [t[n : n + 1].astype(jnp.int32) for n in range(2)]
        if axis == 1:
            lines = [column(line) for line in lines]
        return ((at == lines[0]) | (at == lines[1])).astype(F32).astype(BF)

    def all_slots(at):
        return at

    def pair_slots(at):
        step = sum((at >= n * CAP).astype(jnp.int32) for n in range(1, SIDE))
        return at + (step + pair) * CAP

    for b in range(2):
        t = trows[y * 2 + b]
        gmat[b] = hits(t, 1, EXPERTS * CAP, all_slots)
        gmat_t[b] = hits(t, 0, EXPERTS * CAP, all_slots)
        for n in range(SIDE):
            t = trows[n * 2 + b]
            gy[b, n] = hits(t, 1, SIDE * CAP, pair_slots)
            gy_t[b, n] = hits(t, 0, SIDE * CAP, pair_slots)


    weights[0].wait()
    weights[1].wait()

    def second(h, i):
        k = chunk(i)
        t = h * NK + k
        j = core * NK + k

        def do_y(ky):
            wait_bytes(ybuf.at[ky, h], f_recv.at[t])
            for n in range(SIDE):
                packed = dot(gy_t[h, n], ybuf[ky, h, n], 1, 0).astype(BF)
                ysend[ky, h, :, n] = packed.reshape(SIDE, CAP, CH)
            dst = rows.at[h, z, :, :, feat(j)]

            def out(o):
                to = (z + o) % SIDE
                send_to(ysend.at[ky, h, to], dst, d_send.at[t], d_recv.at[t], at_z(to))

            others(out)
            pltpu.make_async_copy(ysend.at[ky, h, z], dst, d_recv.at[t]).start()

        def do_z(kz):
            wait_bytes(zbuf.at[kz, h], f_recv.at[t])
            dst = rows.at[h, :, y, :, feat(j)]

            def out(o):
                to = (y + o) % SIDE
                send_to(
                    zbuf.at[kz, h, :, to // 2], dst, d_send.at[t], d_recv.at[t], at_y(to)
                )

            others(out)
            pltpu.make_async_copy(zbuf.at[kz, h, :, pair], dst, d_recv.at[t]).start()

        by_type(i, do_y, do_z)

    def forward(f):
        h = f // 4
        c4 = (f % 4) * 4
        stash(f).wait()

        def dequant(q, _):
            chp = c4 + q
            sc = scale_t[pl.ds(pl.multiple_of((chp * 2 + h) * CAP, CAP), CAP), :]
            for n in range(D // 128):
                cols = slice(n * 128, (n + 1) * 128)
                v = inputs[h, chp, :, cols].astype(F32) * sc[:, n : n + 1]
                inputs[h, chp, :, cols] = v.astype(BF)
            return 0

        lax.fori_loop(0, 4, dequant, 0)
        at = pl.ds(pl.multiple_of(f * 4 * CAP, 4 * CAP), 4 * CAP)
        both = dot(inputs[h, pl.ds(c4, 4)].reshape(4 * CAP, D), wgu[...], 1, 0)
        ga[at] = both[:, :FD]
        gb[at] = both[:, FD:]

    def dispatch(i):
        first(0, i)

        @pl.when((core == 1) & (i == 2))
        def _():
            loop(0, NK, xs)

        forward(i)
        second(0, i - 1)

    forward(0)
    loop(1, NK, dispatch)
    second(0, NK - 1)
    loop(0, NK, lambda i: first(1, i))
    forward(NK)

    wait_bytes(grecv, g_recv)
    diag = lax.broadcasted_iota(jnp.int32, (CAP, TOK), 0) == lax.broadcasted_iota(
        jnp.int32, (CAP, TOK), 1
    )

    def factors(b, _):
        at = pl.ds(pl.multiple_of(b * CAP, CAP), CAP)
        source = (b % NCHIP) * 2 + b // NCHIP
        w = jnp.sum(jnp.where(diag, grecv[source][0:1], 0.0), axis=1, keepdims=True)
        g = ga[at]
        u = gb[at]
        sigma = jax.nn.sigmoid(g)
        swish = g * sigma
        h = swish * u
        hid[at] = h
        sh[at] = (w * h).astype(BF)
        ga[at] = w * u * sigma * (1.0 + g * (1.0 - sigma))
        gb[at] = w * swish
        return 0

    lax.fori_loop(0, NDEV, factors, 0)

    def pass_on(h, i):
        k = chunk(i)
        t = h * NK + k
        mine = block(h, core * NK + k)
        wait_bytes(mine, d_recv.at[t])
        send_to(mine, mine, s_send.at[t], s_recv.at[t], sib)

    def settle(h, i):
        k = chunk(i)
        wait_bytes(block(h, other * NK + k), s_recv.at[h * NK + k])

    def pre(h, zz):
        at = pl.ds(pl.multiple_of(h * HSLOTS + zz * SIDE * CAP, SIDE * CAP), SIDE * CAP)
        r = dot(rows[h, zz].reshape(SIDE * CAP, D), wd[...], 1, 1)
        dgu[at, 0:FD] = (r * ga[at]).astype(BF)
        dgu[at, FD : 2 * FD] = (r * gb[at]).astype(BF)
        part = jnp.sum(r * hid[at], axis=1, keepdims=True)
        for n in range(SIDE):
            piece = part[n * CAP : (n + 1) * CAP]
            line = jnp.sum(jnp.where(diag, piece, 0.0), axis=0, keepdims=True)
            gpsend[(zz * SIDE + n) * 2 + h] = jnp.broadcast_to(line, (8, TOK))

    def partial_of(h, j, r):
        at = pl.ds(pl.multiple_of(h * HSLOTS + r * PART, PART), PART)
        return dot(dgu[at], wgu[feat(j)], 1, 1)

    def to_sibling(h, i):
        k = chunk(i)
        turn = h * NK + i
        slot = turn % 2

        @pl.when(turn >= 2)
        def _():
            wait_bytes(psend.at[slot], p_send.at[slot])

        def part(r, _):
            psend[slot, pl.ds(r * 2, 2)] = (
                partial_of(h, other * NK + k, r).astype(BF).reshape(2, SIDE, CAP, CH)
            )
            return 0

        lax.fori_loop(0, 2, part, 0)
        send_to(
            psend.at[slot], comb.at[h, k], p_send.at[slot], p_recv.at[h * NK + k], sib
        )

    def combine(h, i):
        k = chunk(i)
        t = h * NK + k

        @pl.when(i + 1 < NK)
        def _():
            to_sibling(h, i + 1)

        wait_bytes(comb.at[h, k], p_recv.at[t])

        def part(r, _):
            got = comb[h, k, pl.ds(r * 2, 2)].reshape(PART, CH).astype(F32)
            comb[h, k, pl.ds(r * 2, 2)] = (
                (partial_of(h, core * NK + k, r) + got).astype(BF).reshape(2, SIDE, CAP, CH)
            )
            return 0

        lax.fori_loop(0, 2, part, 0)

        def do_y(ky):
            dst = ybk.at[h, ky, z]

            def out(o):
                to = (z + o) % SIDE
                send_to(comb.at[h, k, to], dst, q_send.at[t], q_recv.at[t], at_z(to))

            others(out)
            pltpu.make_async_copy(comb.at[h, k, z], dst, q_recv.at[t]).start()

        def do_z(kz):
            dst = cbuf.at[h, kz, y]

            def out(o):
                to = (y + o) % SIDE
                send_to(comb.at[h, k, :, to], dst, q_send.at[t], q_recv.at[t], at_y(to))

            others(out)
            pltpu.make_async_copy(comb.at[h, k, :, y], dst, q_recv.at[t]).start()

        by_type(i, do_y, do_z)

    def relay(h, i):
        t = h * NK + chunk(i)

        def do_y(ky):
            wait_bytes(ybk.at[h, ky], q_recv.at[t])
            for n in range(SIDE):
                mat = ybk[h, ky, :, n].reshape(SIDE * CAP, CH)
                ybuf[ky, h, n] = dot(gy[h, n], mat, 1, 0).astype(BF)
            dst = ytok.at[h, ky, y]

            def out(o):
                to = (y + o) % SIDE
                send_to(ybuf.at[ky, h, to], dst, c_send.at[t], c_recv.at[t], at_y(to))

            others(out)
            pltpu.make_async_copy(ybuf.at[ky, h, y], dst, c_recv.at[t]).start()

        def do_z(kz):
            wait_bytes(cbuf.at[h, kz], q_recv.at[t])
            wait_bytes(comb.at[0, 0, pl.ds(0, SIDE - 1)], d_send.at[t])
            for n in range(2):
                total = cbuf[h, kz, 2 * n].astype(F32) + cbuf[h, kz, 2 * n + 1].astype(F32)
                zbuf[kz, h, :, n] = total.astype(BF)
            dst = backz.at[h, kz, z]

            def out(o):
                to = (z + o) % SIDE
                send_to(zbuf.at[kz, h, to], dst, c_send.at[t], c_recv.at[t], at_z(to))

            others(out)
            pltpu.make_async_copy(zbuf.at[kz, h, z], dst, c_recv.at[t]).start()

        by_type(i, do_y, do_z)

    def outs(slot, j):
        return (
            pltpu.make_async_copy(st_d.at[slot], gwd_h.at[:, feat(j)], o_sem.at[0, slot]),
            pltpu.make_async_copy(st_g.at[slot], gwg_h.at[feat(j)], o_sem.at[1, slot]),
            pltpu.make_async_copy(st_u.at[slot], gwu_h.at[feat(j)], o_sem.at[2, slot]),
        )

    def wgrad(j):
        slot = j % 2

        @pl.when(j >= 2)
        def _():
            for copy in outs(slot, j - 2):
                copy.wait()

        st_d[slot] = dot(sh[...], rows[:, :, :, :, feat(j)].reshape(SLOTS, CH), 0, 0).astype(BF)
        xin = inputs[:, :, :, feat(j)].reshape(SLOTS, CH)
        both = dot(xin, dgu[...], 0, 0)
        st_g[slot] = both[:, :FD].astype(BF)
        st_u[slot] = both[:, FD:].astype(BF)
        for copy in outs(slot, j):
            copy.start()

    def send_part(o):
        to = (me + o) % NDEV
        send_to(gpsend.at[to], gprecv.at[me], gp_send, gp_recv, to)

    loop(0, NK, lambda i: pass_on(0, i), lambda i: second(1, i))
    weights[2].wait()
    loop(0, NK, lambda i: settle(0, i))
    loop(0, SIDE, lambda n: pre(0, n))
    to_sibling(0, 0)
    loop(0, NK, lambda i: combine(0, i), lambda i: pass_on(1, i))
    loop(0, NK, lambda i: settle(1, i))
    loop(0, SIDE, lambda n: pre(1, n))
    to_sibling(1, 0)
    loop(0, NK, lambda i: combine(1, i), lambda i: relay(0, i))
    loop(1, NDEV, send_part)
    pltpu.make_async_copy(gpsend.at[me], gprecv.at[me], gp_recv).start()
    loop(
        0, NK, lambda i: wgrad(2 * i), lambda i: relay(1, i), lambda i: wgrad(2 * i + 1)
    )
    for j in (2 * NK - 2, 2 * NK - 1):
        for copy in outs(j % 2, j):
            copy.wait()

    def final(h, i):
        k = chunk(i)
        t = h * NK + k

        def hand(got):
            @pl.when(core == h)
            def _():
                gout[core * NK + k] = got

            @pl.when(core != h)
            def _():
                gsib[k] = got
                send_to(gsib.at[k], gout.at[core * NK + k], gi_send, gi_recv.at[k], sib)

        def do_y(ky):
            wait_bytes(ytok.at[h, ky], c_recv.at[t])
            hand(sum(ytok[h, ky, n].astype(F32) for n in range(SIDE)).astype(BF))

        def do_z(kz):
            wait_bytes(backz.at[h, kz], c_recv.at[t])
            mat = backz[h, kz].reshape(EXPERTS * CAP, CH)
            hand(dot(gmat[h], mat, 1, 0).astype(BF))

        by_type(i, do_y, do_z)

    for h in range(2):

        def finals(k, _):
            final(h, k)
            return 0

        lax.fori_loop(0, NK, finals, 0)

    def put(j):
        return pltpu.make_async_copy(
            gout.at[j], gi_h.at[:, pl.ds(pl.multiple_of(j * CH, CH), CH)], go_sem.at[j]
        )

    def write(k, _):
        put(core * NK + k).start()
        return 0

    lax.fori_loop(0, NK, write, 0)

    wait_bytes(gprecv, gp_recv)
    acc0 = jnp.zeros((TOK, TOK), F32)
    acc1 = jnp.zeros((TOK, TOK), F32)
    for e in range(EXPERTS):
        total = (
            gprecv[4 * e][0:1] + gprecv[4 * e + 1][0:1]
            + gprecv[4 * e + 2][0:1] + gprecv[4 * e + 3][0:1]
        )
        at = lane + e * CAP
        inside = lane < CAP
        acc0 = acc0 + jnp.where((at == tgt[0]) & inside, total, 0.0)
        acc1 = acc1 + jnp.where((at == tgt[1]) & inside, total, 0.0)
    for n, acc in enumerate((acc0, acc1)):
        part = jnp.sum(acc, axis=1, keepdims=True)
        gg_o[n : n + 1, :] = jnp.sum(jnp.where(same, part, 0.0), axis=0, keepdims=True)

    def write_sib(k, _):
        wait_bytes(gout.at[other * NK + k], gi_recv.at[k])
        put(other * NK + k).start()
        return 0

    lax.fori_loop(0, NK, write_sib, 0)

    wait_bytes(xbuf, x_send)
    wait_bytes(trows.at[pl.ds(0, 7)], t_send)
    wait_bytes(grecv.at[pl.ds(0, NDEV - 1)], g_send)
    wait_bytes(gprecv.at[pl.ds(0, NDEV - 1)], gp_send)
    wait_bytes(gsib, gi_send)

    def drain(t, _):
        wait_bytes(comb.at[0, 0, pl.ds(0, SIDE - 1)], q_send.at[t])
        wait_bytes(comb.at[0, 0], s_send.at[t])

        @pl.when(t % NK >= NZ)
        def _():
            wait_bytes(comb.at[0, 0, pl.ds(0, SIDE - 1)], d_send.at[t])
            wait_bytes(ybuf.at[0, 0, pl.ds(0, SIDE - 1)], f_send.at[t])
            wait_bytes(ybuf.at[0, 0, pl.ds(0, SIDE - 1)], c_send.at[t])

        @pl.when(t % NK < NZ)
        def _():
            wait_bytes(zbuf.at[0, 0, pl.ds(0, SIDE - 1)], f_send.at[t])
            wait_bytes(zbuf.at[0, 0, pl.ds(0, SIDE - 1)], c_send.at[t])

        put(t).wait()
        return 0

    lax.fori_loop(0, 2 * NK, drain, 0)
    for slot in range(2):
        wait_bytes(psend.at[slot], p_send.at[slot])


def emit(*refs):
    count = (len(refs) - 1) // 3
    srcs, dsts, bufs, sem = refs[:count], refs[count : 2 * count], refs[2 * count : -1], refs[-1]
    loads, stores = [], []
    n = 0
    for src, dst, buf in zip(srcs, dsts, bufs):
        size = src.shape[0]
        pieces = 4 if size >= 64 else 1
        for p in range(pieces):
            at = pl.ds(p * (size // pieces), size // pieces)
            loads.append(pltpu.make_async_copy(src.at[at], buf.at[at], sem.at[0, n]))
            stores.append(pltpu.make_async_copy(buf.at[at], dst.at[at], sem.at[1, n]))
            n += 1
    for load in loads:
        load.start()
    for load, store in zip(loads, stores):
        load.wait()
        store.start()
    for store in stores:
        store.wait()


def local(nsec, upstream, routes, gates, w_gate, w_up, w_down, stash_q, stash_scale):
    hbm = pl.BlockSpec(memory_space=pl.ANY)
    vmem = pl.BlockSpec(memory_space=pltpu.VMEM)
    dma = pltpu.SemaphoreType.DMA
    v = pltpu.VMEM
    both = 2 * NK
    scratch = [
        v((2, SIDE, SIDE, CAP, D), BF),
        v((2, NCHIP, CAP, D), BF),
        v((D, 2 * FD), BF), v((FD, D), BF),
        v((SLOTS, FD), F32), v((SLOTS, FD), F32), v((SLOTS, FD), F32),
        v((SLOTS, FD), BF), v((SLOTS, 2 * FD), BF),
        v((NZ, 2, SIDE, 2, CAP, CH), BF), v((NZ, 2, SIDE, 2, CAP, CH), BF),
        v((NY, 2, SIDE, TOK, CH), BF), v((NY, 2, SIDE, SIDE, CAP, CH), BF),
        v((NK, 2, TOK, CH), BF),
        v((2, NK, SIDE, SIDE, CAP, CH), BF),
        v((2, SIDE, SIDE, CAP, CH), BF),
        v((2, NZ, SIDE, SIDE, CAP, CH), BF), v((2, NZ, SIDE, 2, CAP, CH), BF),
        v((2, NY, SIDE, SIDE, CAP, CH), BF), v((2, NY, SIDE, TOK, CH), BF),
        v((both, TOK, CH), BF), v((NK, TOK, CH), BF),
        v((D // 128, 1, SLOTS), F32), v((SLOTS, 32), F32),
        v((2, TOK, EXPERTS * CAP), BF), v((2, EXPERTS * CAP, TOK), BF),
        v((2, SIDE, TOK, SIDE * CAP), BF), v((2, SIDE, SIDE * CAP, TOK), BF),
        v((2, TOK, TOK), jnp.int32),
        v((8, TOK), F32), v((8, 8, TOK), F32),
        v((EXPERTS, 8, TOK), F32), v((NDEV, 8, TOK), F32),
        v((NDEV, 8, TOK), F32), v((NDEV, 8, TOK), F32),
        v((2, FD, CH), BF), v((2, CH, FD), BF), v((2, CH, FD), BF),
        dma, dma((both,)), dma((both,)), dma((both,)), dma((both,)), dma((both,)),
        dma((both,)), dma((both,)), dma((2,)), dma((both,)), dma((both,)), dma((both,)),
        dma((both,)), dma((both,)), dma, dma, dma, dma, dma, dma,
        dma, dma((NK,)), dma((3,)), dma((NFR,)), dma, dma((3, 2)), dma((both,)),
    ]
    shapes = (
        jax.ShapeDtypeStruct((TOK, D), BF),
        jax.ShapeDtypeStruct((2, TOK), F32),
        jax.ShapeDtypeStruct((D, FD), BF),
        jax.ShapeDtypeStruct((D, FD), BF),
        jax.ShapeDtypeStruct((FD, D), BF),
    )
    out = pl.pallas_call(
        functools.partial(kernel, nsec),
        out_shape=shapes,
        in_specs=[vmem, vmem] + [hbm] * 6,
        out_specs=(hbm, vmem, hbm, hbm, hbm),
        scratch_shapes=scratch,
        compiler_params=pltpu.CompilerParams(
            collective_id=0, has_side_effects=True, vmem_limit_bytes=67_043_328
        ),
    )(
        routes[0].T, gates[0].T, upstream[0], w_gate[0], w_up[0], w_down[0],
        stash_q.reshape(NCHIP, 2, CAP, D), jnp.transpose(stash_scale, (2, 0, 1)),
    )
    out = pl.pallas_call(
        emit,
        out_shape=shapes,
        in_specs=[hbm] * 5,
        out_specs=(hbm,) * 5,
        scratch_shapes=[v(o.shape, o.dtype) for o in shapes] + [dma((2, 20))],
        compiler_params=pltpu.CompilerParams(vmem_limit_bytes=64_000_000),
    )(*out)
    gi, gg, gwg, gwu, gwd = out
    return gi[None], gg.T[None], gwg[None], gwu[None], gwd[None]


def solution(mesh):
    three = P("section", "expert", None)
    cols = P("section", None, "expert")
    return jax.shard_map(
        functools.partial(local, mesh.shape["section"]),
        mesh=mesh,
        in_specs=(three, three, three, cols, cols, three, three, three),
        out_specs=(three, three, cols, cols, three),
        check_vma=False,
    )
```

time: 146 us -> 127 us (0.87)
  Pallas kernels: 145 us -> 127 us
    pallas_call x1, Pallas kernels: 140 us -> 121 us  [local(): pl.pallas_call(functools.partial(kernel, nsec), out_shape=shapes, in_spec...]
where the time goes in v2:
time: 127 us
  Pallas kernels  127 us (100%)
    pallas_call x1, Pallas kernels, local(): pl.pallas_call(functools.partial(kernel, nsec), out_shape=shapes, in_spec...  121 us
    pallas_call x1, Pallas kernels, local(): pl.pallas_call(emit, out_shape=shapes, in_specs=[hbm] * 5, out_specs=(hbm...  5.56 us

profile of v2, /device:TPU:1, one launch (start us, length us, event | category | flops | bytes accessed | tf_op | source)
XLA Modules:
  0.0 127.4 jit_solution(4518998746645055675)
XLA Ops:
  0.6 121.2 %shard_map.119 = (bf16[128,3584]{1,0:T(8,128)(2,1)}, f32[2,128]{1,0:T(2,128)}, bf16[3584,256]{1,0:T(8,128)(2,1)}, bf16[3584,256]{1,0:T(8,128)(2,1)}, bf16[256,3584]{1,0:T(8,128)(2,1)}) custom-call(s32[2,128]{1,0:T(2,128)} %bitcast.25, f32[2,128]{1,0:T(2,128)} %bitcast.26, bf16[128,3584]{1,0:T(8,128)(2,1)} %bitcast.23, bf16[3584,256]{1,0:T(8,128)(2,1)} %bitcast.20, ...), custom_call_target="tpu_custom_call" | custom-call | tf_op jit(solution)/shard_map/pallas_call | solution.py:699
  121.8 5.6 %shard_map.120 = (bf16[128,3584]{1,0:T(8,128)(2,1)}, f32[2,128]{1,0:T(2,128)}, bf16[3584,256]{1,0:T(8,128)(2,1)}, bf16[3584,256]{1,0:T(8,128)(2,1)}, bf16[256,3584]{1,0:T(8,128)(2,1)}) custom-call(bf16[128,3584]{1,0:T(8,128)(2,1)} %get-tuple-element.15.refs_0_, f32[2,128]{1,0:T(2,128)} %get-tuple-element.16.refs_1_, ...), custom_call_target="tpu_custom_call" | custom-call | tf_op jit(solution)/shard_map/pallas_call | solution.py:712

commit v3 on v2

--- a/solution.py
+++ b/solution.py
@@ -39,15 +39,15 @@
 
 def kernel(
     nsec,
-    routes, gates, up, wg_h, wu_h, wd_h, sq_h, ss_h,
+    routes_h, gates_h, up, wg_h, wu_h, wd_h, sq_h, ss_h,
     gi_h, gg_o, gwg_h, gwu_h, gwd_h,
-    rows, inputs, wgu, wd, ga, gb, hid, sh, dgu,
+    routes, gates, rows, inputs, wgu, wd, ga, gb, hid, sh, dgu,
     zsend, zbuf, ybuf, ysend, xbuf, comb, psend, cbuf, backz, ybk, ytok, gout, gsib,
     scale, scale_t, gmat, gmat_t, gy, gy_t, tgt, trow, trows,
     gsend, grecv, gpsend, gprecv, st_d, st_g, st_u,
     x_send, x_recv, f_send, f_recv, d_send, d_recv, s_send, s_recv, p_send, p_recv,
     q_send, q_recv, c_send, c_recv, t_send, t_recv, g_send, g_recv, gp_send, gp_recv,
-    gi_send, gi_recv, w_sem, sq_sem, ss_sem, o_sem, go_sem,
+    gi_send, gi_recv, w_sem, sq_sem, ss_sem, o_sem, go_sem, l_sem,
 ):
     sec = lax.axis_index("section")
     me = lax.axis_index("expert")
@@ -110,6 +110,27 @@
         def _():
             do_z(i // 2)
 
+    bar = pltpu.get_barrier_semaphore()
+
+    def greet(o, _):
+        pl.semaphore_signal(
+            bar, inc=1, device_id=(sec, (me + o) % NDEV), device_id_type=MESH
+        )
+        return 0
+
+    lax.fori_loop(1, NDEV, greet, 0)
+    for sx in (down, upper):
+        for cc in range(2):
+            pl.semaphore_signal(
+                bar, inc=1, device_id=(sx, chip * 2 + cc), device_id_type=MESH
+            )
+
+    small = (
+        pltpu.make_async_copy(routes_h, routes, l_sem.at[0]),
+        pltpu.make_async_copy(gates_h, gates, l_sem.at[1]),
+    )
+    for copy in small:
+        copy.start()
     pltpu.make_async_copy(ss_h, scale, ss_sem).start()
 
     def stash(f):
@@ -129,20 +150,26 @@
     for copy in weights:
         copy.start()
 
-    bar = pltpu.get_barrier_semaphore()
-
-    def greet(o, _):
-        pl.semaphore_signal(
-            bar, inc=1, device_id=(sec, (me + o) % NDEV), device_id_type=MESH
-        )
-        return 0
-
-    lax.fori_loop(1, NDEV, greet, 0)
-    for sx in (down, upper):
+    pl.semaphore_wait(bar, NDEV - 1 + 4)
+
+    def xs(i):
+        k = chunk(i)
         for cc in range(2):
-            pl.semaphore_signal(
-                bar, inc=1, device_id=(sx, chip * 2 + cc), device_id_type=MESH
-            )
+            pltpu.make_async_remote_copy(
+                src_ref=up.at[:, pl.ds(pl.multiple_of(cc * HALF + k * CH, CH), CH)],
+                dst_ref=xbuf.at[k, core],
+                send_sem=x_send,
+                recv_sem=x_recv.at[core * NK + k],
+                device_id=(down, chip * 2 + cc),
+                device_id_type=MESH,
+            ).start()
+
+    @pl.when(core == 0)
+    def _():
+        loop(0, NK, xs)
+
+    for copy in small:
+        copy.wait()
 
     lane = lax.broadcasted_iota(jnp.int32, (TOK, TOK), 1)
     sub = lax.broadcasted_iota(jnp.int32, (TOK, TOK), 0)
@@ -173,24 +200,6 @@
         hit = jnp.where((at == t0) & inside, w0, 0.0) + jnp.where((at == t1) & inside, w1, 0.0)
         gsend[e] = jnp.broadcast_to(jnp.sum(hit, axis=0, keepdims=True), (8, TOK))
 
-    pl.semaphore_wait(bar, NDEV - 1 + 4)
-
-    def xs(i):
-        k = chunk(i)
-        for cc in range(2):
-            pltpu.make_async_remote_copy(
-                src_ref=up.at[:, pl.ds(pl.multiple_of(cc * HALF + k * CH, CH), CH)],
-                dst_ref=xbuf.at[k, core],
-                send_sem=x_send,
-                recv_sem=x_recv.at[core * NK + k],
-                device_id=(down, chip * 2 + cc),
-                device_id_type=MESH,
-            ).start()
-
-    @pl.when(core == 0)
-    def _():
-        loop(0, NK, xs)
-
     spot = me % 8
 
     def send_rows(o, _):
@@ -241,14 +250,6 @@
 
     first(0, 0)
 
-    pltpu.make_async_copy(ss_h, scale, ss_sem).wait()
-    for q in range(4):
-        for m in range(3):
-            at = slice(q * 384 + m * 128, q * 384 + (m + 1) * 128)
-            lines = [scale[n, :, at] for n in range(D // 128)]
-            lines.append(jnp.zeros((4, 128), F32))
-            scale_t[at, :] = jnp.concatenate(lines, axis=0).T
-
     wait_bytes(trows, t_recv)
 
     def hits(t, axis, size, positions):
@@ -267,17 +268,10 @@
         return at + (step + pair) * CAP
 
     for b in range(2):
-        t = trows[y * 2 + b]
-        gmat[b] = hits(t, 1, EXPERTS * CAP, all_slots)
-        gmat_t[b] = hits(t, 0, EXPERTS * CAP, all_slots)
+        gmat_t[b] = hits(trows[y * 2 + b], 0, EXPERTS * CAP, all_slots)
         for n in range(SIDE):
-            t = trows[n * 2 + b]
-            gy[b, n] = hits(t, 1, SIDE * CAP, pair_slots)
-            gy_t[b, n] = hits(t, 0, SIDE * CAP, pair_slots)
-
-
-    weights[0].wait()
-    weights[1].wait()
+            gy_t[b, n] = hits(trows[n * 2 + b], 0, SIDE * CAP, pair_slots)
+
 
     def second(h, i):
         k = chunk(i)
@@ -333,21 +327,37 @@
         ga[at] = both[:, :FD]
         gb[at] = both[:, FD:]
 
-    def dispatch(i):
-        first(0, i)
-
-        @pl.when((core == 1) & (i == 2))
-        def _():
-            loop(0, NK, xs)
-
-        forward(i)
-        second(0, i - 1)
-
+    loop(1, 5, lambda i: first(0, i))
+
+    @pl.when(core == 1)
+    def _():
+        loop(0, NK, xs)
+
+    second(0, 0)
+
+    pltpu.make_async_copy(ss_h, scale, ss_sem).wait()
+    for q in range(4):
+        for m in range(3):
+            at = slice(q * 384 + m * 128, q * 384 + (m + 1) * 128)
+            lines = [scale[n, :, at] for n in range(D // 128)]
+            lines.append(jnp.zeros((4, 128), F32))
+            scale_t[at, :] = jnp.concatenate(lines, axis=0).T
+
+    for b in range(2):
+        gmat[b] = hits(trows[y * 2 + b], 1, EXPERTS * CAP, all_slots)
+        for n in range(SIDE):
+            gy[b, n] = hits(trows[n * 2 + b], 1, SIDE * CAP, pair_slots)
+    weights[0].wait()
+    weights[1].wait()
+    first(0, 5)
+    second(0, 1)
     forward(0)
-    loop(1, NK, dispatch)
-    second(0, NK - 1)
-    loop(0, NK, lambda i: first(1, i))
-    forward(NK)
+    first(0, 6)
+    second(0, 2)
+    forward(1)
+    loop(3, NK, lambda i: second(0, i), lambda i: first(1, i - 3), lambda i: forward(i - 1))
+    loop(4, NK, lambda i: first(1, i))
+    loop(6, NFR, forward)
 
     wait_bytes(grecv, g_recv)
     diag = lax.broadcasted_iota(jnp.int32, (CAP, TOK), 0) == lax.broadcasted_iota(
@@ -663,6 +673,7 @@
     v = pltpu.VMEM
     both = 2 * NK
     scratch = [
+        v((2, TOK), jnp.int32), v((2, TOK), F32),
         v((2, SIDE, SIDE, CAP, D), BF),
         v((2, NCHIP, CAP, D), BF),
         v((D, 2 * FD), BF), v((FD, D), BF),
@@ -688,6 +699,7 @@
         dma((both,)), dma((both,)), dma((2,)), dma((both,)), dma((both,)), dma((both,)),
         dma((both,)), dma((both,)), dma, dma, dma, dma, dma, dma,
         dma, dma((NK,)), dma((3,)), dma((NFR,)), dma, dma((3, 2)), dma((both,)),
+        dma((2,)),
     ]
     shapes = (
         jax.ShapeDtypeStruct((TOK, D), BF),
@@ -699,7 +711,7 @@
     out = pl.pallas_call(
         functools.partial(kernel, nsec),
         out_shape=shapes,
-        in_specs=[vmem, vmem] + [hbm] * 6,
+        in_specs=[hbm] * 8,
         out_specs=(hbm, vmem, hbm, hbm, hbm),
         scratch_shapes=scratch,
         compiler_params=pltpu.CompilerParams(

time: 127 us -> 124 us (0.976)
  Pallas kernels: 127 us -> 123 us
    pallas_call x1, Pallas kernels: 121 us -> 118 us  [local(): pl.pallas_call(functools.partial(kernel, nsec), out_shape=shapes, in_spec...]
where the time goes in v3:
time: 124 us
  Pallas kernels  123 us (99%)
    pallas_call x1, Pallas kernels, local(): pl.pallas_call(functools.partial(kernel, nsec), out_shape=shapes, in_spec...  118 us
    pallas_call x1, Pallas kernels, local(): pl.pallas_call(emit, out_shape=shapes, in_specs=[hbm] * 5, out_specs=(hbm...  5.56 us

profile of v3, /device:TPU:1, one launch (start us, length us, event | category | flops | bytes accessed | tf_op | source)
XLA Modules:
  0.0 123.9 jit_solution(4580670800409865145)
XLA Ops:
  0.6 117.7 %shard_map.119 = (bf16[128,3584]{1,0:T(8,128)(2,1)}, f32[2,128]{1,0:T(2,128)}, bf16[3584,256]{1,0:T(8,128)(2,1)}, bf16[3584,256]{1,0:T(8,128)(2,1)}, bf16[256,3584]{1,0:T(8,128)(2,1)}) custom-call(s32[2,128]{1,0:T(2,128)} %bitcast.25, f32[2,128]{1,0:T(2,128)} %bitcast.26, bf16[128,3584]{1,0:T(8,128)(2,1)} %bitcast.23, bf16[3584,256]{1,0:T(8,128)(2,1)} %bitcast.20, ...), custom_call_target="tpu_custom_call" | custom-call | tf_op jit(solution)/shard_map/pallas_call | solution.py:711
  118.4 5.6 %shard_map.120 = (bf16[128,3584]{1,0:T(8,128)(2,1)}, f32[2,128]{1,0:T(2,128)}, bf16[3584,256]{1,0:T(8,128)(2,1)}, bf16[3584,256]{1,0:T(8,128)(2,1)}, bf16[256,3584]{1,0:T(8,128)(2,1)}) custom-call(bf16[128,3584]{1,0:T(8,128)(2,1)} %get-tuple-element.15.refs_0_, f32[2,128]{1,0:T(2,128)} %get-tuple-element.16.refs_1_, ...), custom_call_target="tpu_custom_call" | custom-call | tf_op jit(solution)/shard_map/pallas_call | solution.py:724

commit v4 on v3

--- a/solution.py
+++ b/solution.py
@@ -39,9 +39,9 @@
 
 def kernel(
     nsec,
-    routes_h, gates_h, up, wg_h, wu_h, wd_h, sq_h, ss_h,
+    routes_h, gates_h, up_h, wg_h, wu_h, wd_h, sq_h, ss_h,
     gi_h, gg_o, gwg_h, gwu_h, gwd_h,
-    routes, gates, rows, inputs, wgu, wd, ga, gb, hid, sh, dgu,
+    routes, gates, up, rows, inputs, wgu, wd, ga, gb, hid, sh, dgu,
     zsend, zbuf, ybuf, ysend, xbuf, comb, psend, cbuf, backz, ybk, ytok, gout, gsib,
     scale, scale_t, gmat, gmat_t, gy, gy_t, tgt, trow, trows,
     gsend, grecv, gpsend, gprecv, st_d, st_g, st_u,
@@ -128,6 +128,7 @@
     small = (
         pltpu.make_async_copy(routes_h, routes, l_sem.at[0]),
         pltpu.make_async_copy(gates_h, gates, l_sem.at[1]),
+        pltpu.make_async_copy(up_h, up, l_sem.at[2]),
     )
     for copy in small:
         copy.start()
@@ -150,26 +151,8 @@
     for copy in weights:
         copy.start()
 
-    pl.semaphore_wait(bar, NDEV - 1 + 4)
-
-    def xs(i):
-        k = chunk(i)
-        for cc in range(2):
-            pltpu.make_async_remote_copy(
-                src_ref=up.at[:, pl.ds(pl.multiple_of(cc * HALF + k * CH, CH), CH)],
-                dst_ref=xbuf.at[k, core],
-                send_sem=x_send,
-                recv_sem=x_recv.at[core * NK + k],
-                device_id=(down, chip * 2 + cc),
-                device_id_type=MESH,
-            ).start()
-
-    @pl.when(core == 0)
-    def _():
-        loop(0, NK, xs)
-
-    for copy in small:
-        copy.wait()
+    small[0].wait()
+    small[1].wait()
 
     lane = lax.broadcasted_iota(jnp.int32, (TOK, TOK), 1)
     sub = lax.broadcasted_iota(jnp.int32, (TOK, TOK), 0)
@@ -200,6 +183,25 @@
         hit = jnp.where((at == t0) & inside, w0, 0.0) + jnp.where((at == t1) & inside, w1, 0.0)
         gsend[e] = jnp.broadcast_to(jnp.sum(hit, axis=0, keepdims=True), (8, TOK))
 
+    small[2].wait()
+    pl.semaphore_wait(bar, NDEV - 1 + 4)
+
+    def xs(i):
+        k = chunk(i)
+        for cc in range(2):
+            pltpu.make_async_remote_copy(
+                src_ref=up.at[:, pl.ds(pl.multiple_of(cc * HALF + k * CH, CH), CH)],
+                dst_ref=xbuf.at[k, core],
+                send_sem=x_send,
+                recv_sem=x_recv.at[core * NK + k],
+                device_id=(down, chip * 2 + cc),
+                device_id_type=MESH,
+            ).start()
+
+    @pl.when(core == 0)
+    def _():
+        loop(0, NK, xs)
+
     spot = me % 8
 
     def send_rows(o, _):
@@ -327,13 +329,16 @@
         ga[at] = both[:, :FD]
         gb[at] = both[:, FD:]
 
-    loop(1, 5, lambda i: first(0, i))
+    loop(1, 3, lambda i: first(0, i))
+    second(0, 0)
+    first(0, 3)
 
     @pl.when(core == 1)
     def _():
         loop(0, NK, xs)
 
-    second(0, 0)
+    first(0, 4)
+    second(0, 1)
 
     pltpu.make_async_copy(ss_h, scale, ss_sem).wait()
     for q in range(4):
@@ -350,7 +355,6 @@
     weights[0].wait()
     weights[1].wait()
     first(0, 5)
-    second(0, 1)
     forward(0)
     first(0, 6)
     second(0, 2)
@@ -673,7 +677,7 @@
     v = pltpu.VMEM
     both = 2 * NK
     scratch = [
-        v((2, TOK), jnp.int32), v((2, TOK), F32),
+        v((2, TOK), jnp.int32), v((2, TOK), F32), v((TOK, D), BF),
         v((2, SIDE, SIDE, CAP, D), BF),
         v((2, NCHIP, CAP, D), BF),
         v((D, 2 * FD), BF), v((FD, D), BF),
@@ -699,7 +703,7 @@
         dma((both,)), dma((both,)), dma((2,)), dma((both,)), dma((both,)), dma((both,)),
         dma((both,)), dma((both,)), dma, dma, dma, dma, dma, dma,
         dma, dma((NK,)), dma((3,)), dma((NFR,)), dma, dma((3, 2)), dma((both,)),
-        dma((2,)),
+        dma((3,)),
     ]
     shapes = (
         jax.ShapeDtypeStruct((TOK, D), BF),

time: 124 us -> 127 us (1.024)
  Pallas kernels: 123 us -> 126 us
    pallas_call x1, Pallas kernels: 118 us -> 120 us  [local(): pl.pallas_call(functools.partial(kernel, nsec), out_shape=shapes, in_spec...]
where the time goes in v4:
time: 127 us
  Pallas kernels  126 us (99%)
    pallas_call x1, Pallas kernels, local(): pl.pallas_call(functools.partial(kernel, nsec), out_shape=shapes, in_spec...  120 us
    pallas_call x1, Pallas kernels, local(): pl.pallas_call(emit, out_shape=shapes, in_specs=[hbm] * 5, out_specs=(hbm...  5.56 us

profile of v4, /device:TPU:1, one launch (start us, length us, event | category | flops | bytes accessed | tf_op | source)
XLA Modules:
  0.0 126.5 jit_solution(18209611505383586812)
XLA Ops:
  0.6 120.3 %shard_map.119 = (bf16[128,3584]{1,0:T(8,128)(2,1)}, f32[2,128]{1,0:T(2,128)}, bf16[3584,256]{1,0:T(8,128)(2,1)}, bf16[3584,256]{1,0:T(8,128)(2,1)}, bf16[256,3584]{1,0:T(8,128)(2,1)}) custom-call(s32[2,128]{1,0:T(2,128)} %bitcast.25, f32[2,128]{1,0:T(2,128)} %bitcast.26, bf16[128,3584]{1,0:T(8,128)(2,1)} %bitcast.23, bf16[3584,256]{1,0:T(8,128)(2,1)} %bitcast.20, ...), custom_call_target="tpu_custom_call" | custom-call | tf_op jit(solution)/shard_map/pallas_call | solution.py:715
  121.0 5.6 %shard_map.120 = (bf16[128,3584]{1,0:T(8,128)(2,1)}, f32[2,128]{1,0:T(2,128)}, bf16[3584,256]{1,0:T(8,128)(2,1)}, bf16[3584,256]{1,0:T(8,128)(2,1)}, bf16[256,3584]{1,0:T(8,128)(2,1)}) custom-call(bf16[128,3584]{1,0:T(8,128)(2,1)} %get-tuple-element.15.refs_0_, f32[2,128]{1,0:T(2,128)} %get-tuple-element.16.refs_1_, ...), custom_call_target="tpu_custom_call" | custom-call | tf_op jit(solution)/shard_map/pallas_call | solution.py:728
